TPU v7x, 32 devices: a whole 2x2x4 slice. The times are simulated.
32 devices in a mesh: fsdp: 8 (over z, core), seq: 4 (over y, x).
Axes of the slice: x: 2, y: 2, z: 4, core: 2. Of those that a mesh axis runs over, the one named last changes fastest.
Arguments:
- tokens: bfloat16 [16384, 2048], P(('fsdp', 'seq')), may hold values from -6 to 6
- mixed_cotangent: bfloat16 [16384, 2048], P(('fsdp', 'seq')), may hold values from -6 to 6
- lengths: int32 [8, 3], P('fsdp'), may hold values from 1 to 1024, 2048 in all within a row
- owner_slot: int32 [16384], P(('fsdp', 'seq')), may hold values from 0 to 16383, as said below
- q_weight: bfloat16 [2048, 2048], P('fsdp'), may hold values from -0.125 to 0.125
- key_projection: bfloat16 [2048, 512], P('fsdp'), may hold values from -0.125 to 0.125
- value_projection: bfloat16 [2048, 512], P('fsdp'), may hold values from -0.125 to 0.125
- out_weight: bfloat16 [2048, 2048], P('fsdp'), may hold values from -1 to 1
- gate_weight: bfloat16 [2048, 8192], P('fsdp'), may hold values from -0.125 to 0.125
- up_weight: bfloat16 [2048, 8192], P('fsdp'), may hold values from -0.125 to 0.125
- down_weight: bfloat16 [2048, 8192], P('fsdp'), may hold values from -0.0625 to 0.0625
- attn_gain: bfloat16 [2048], P('fsdp'), may hold values from 0.25 to 1.75
- ffn_gain: bfloat16 [2048], P('fsdp'), may hold values from 0.25 to 1.75
- query_gain: bfloat16 [64], replicated, may hold values from 0.25 to 1.75
- key_gain: bfloat16 [64], replicated, may hold values from 0.25 to 1.75
Outputs:
- mixed: bfloat16 [16384, 2048], P(('fsdp', 'seq'))
- input_grad: bfloat16 [16384, 2048], P(('fsdp', 'seq'))
- q_weight_grad: float32 [2048, 2048], P('fsdp')
- k_weight_grad: float32 [2048, 512], P('fsdp')
- v_weight_grad: float32 [2048, 512], P('fsdp')
- out_weight_grad: float32 [2048, 2048], P('fsdp')
- gate_weight_grad: float32 [2048, 8192], P('fsdp')
- up_weight_grad: float32 [2048, 8192], P('fsdp')
- down_weight_grad: float32 [2048, 8192], P('fsdp')
- attn_gain_grad: float32 [2048], P('fsdp')
- ffn_gain_grad: float32 [2048], P('fsdp')
- query_gain_grad: float32 [64], replicated
- key_gain_grad: float32 [64], replicated
Inputs may be any that keep to these rules, and one draw needn't show every extreme that they name: owner_slot is a permutation of the token positions. Write a given position p as (f * 4 + s) * 512 + r with r < 512, s < 4; its owner position q is (j * 4 + s) * 512 + f * 64 + t for some j < 8 and t < 64: a token keeps its index s along seq, and each device gives exactly 64 tokens to each owner in its column. lengths[g] lists the sequences of owned group g in order and sums to 2048.
All inputs are finite; a program needn't handle non-finite values.
Results may differ from a plain program's by a relative error of at most 0.022.
Values may be sent and summed in bfloat16 or wider, within the bound.
A program may use at most 512 MiB of HBM per device.

v0:
```python
import math

import jax
import jax.numpy as jnp
from jax import lax
from jax.sharding import PartitionSpec as P

D = 2048
QUERY_HEADS = 32
KEY_VALUE_HEADS = 8
HEAD_SIZE = 64


EPS = 1e-05
THETA = 1000000.0
NEGATIVE = -1e30


def rms_normalize(values, gain_vector):
    return values * lax.rsqrt(jnp.mean(values * values, axis=-1, keepdims=True) + EPS) * gain_vector


def rotary_apply(values, cosine_table, sine_table):
    middle = values.shape[-1] // 2
    first_half = values[..., :middle]
    second_half = values[..., middle:]
    return jnp.concatenate(
        [
            first_half * cosine_table - second_half * sine_table,
            second_half * cosine_table + first_half * sine_table,
        ],
        axis=-1,
    )


def doc_table(lengths_row, offset, number):
    token_spots = offset + jnp.arange(number, dtype=jnp.int32)
    seq_ends = jnp.cumsum(lengths_row)
    passed = token_spots[:, None] >= seq_ends[None, :]
    document_index = jnp.sum(passed.astype(jnp.int32), axis=1)
    starts = jnp.sum(jnp.where(passed, lengths_row[None, :], 0), axis=1)
    return (document_index, (token_spots - starts).astype(jnp.float32))


def rotary_tables(places):
    freqs = jnp.exp(
        jnp.arange(HEAD_SIZE // 2, dtype=jnp.float32) * (-2.0 * math.log(THETA) / HEAD_SIZE)
    )
    angles = places[:, None] * freqs[None, :]
    return (jnp.cos(angles)[:, None, :], jnp.sin(angles)[:, None, :])


def outer_rows(left_rows, right_cols):
    return jnp.einsum("tr,tc->rc", left_rows, right_cols, preferred_element_type=jnp.float32)


def split_wide(shard_terms, widths):
    edges = [0]
    for width_item in widths:
        edges.append(edges[-1] + width_item)
    return [
        shard_terms[:, edges[index_pos] : edges[index_pos + 1]] for index_pos in range(len(widths))
    ]


def body(
    tokens,
    mixed_cotangent,
    lengths,
    owner_slot,
    q_weight,
    key_projection,
    value_projection,
    out_weight,
    gate_weight,
    up_weight,
    down_weight,
    attn_gain,
    ffn_gain,
    query_gain,
    key_gain,
):
    f32 = jnp.float32
    brain_float_half = jnp.bfloat16
    groups = lax.axis_size("fsdp")
    ranks = lax.axis_size("seq")
    token_rows = tokens.shape[0]
    slice_rows = token_rows // groups
    group_width = QUERY_HEADS // KEY_VALUE_HEADS
    score_scale = 1.0 / math.sqrt(HEAD_SIZE)
    local_slot = owner_slot % token_rows
    target = owner_slot // token_rows // ranks
    send_spot = target * slice_rows + local_slot % slice_rows
    inverse = (
        jnp.zeros((token_rows,), jnp.int32)
        .at[send_spot]
        .set(jnp.arange(token_rows, dtype=jnp.int32))
    )
    owned, cot_owned = (
        lax.all_to_all(tokens[inverse], "fsdp", split_axis=0, concat_axis=0, tiled=True),
        lax.all_to_all(mixed_cotangent[inverse], "fsdp", split_axis=0, concat_axis=0, tiled=True),
    )
    wq_full, wk_full, wv_full, wo_full, attn_gain_full = (
        lax.all_gather(q_weight, "fsdp", axis=0, tiled=True),
        lax.all_gather(key_projection, "fsdp", axis=0, tiled=True),
        lax.all_gather(value_projection, "fsdp", axis=0, tiled=True),
        lax.all_gather(out_weight, "fsdp", axis=0, tiled=True),
        lax.all_gather(attn_gain, "fsdp", axis=0, tiled=True),
    )
    lengths_row = lengths[0]
    seq_index = lax.axis_index("seq")
    _, own_places = doc_table(lengths_row, seq_index * token_rows, token_rows)
    cosine_table, sine_table = rotary_tables(own_places)
    tok_f32 = owned.astype(f32)
    normed_f32, norm_one_pull = jax.vjp(rms_normalize, tok_f32, attn_gain_full.astype(f32))
    normalized_rows = normed_f32.astype(brain_float_half)
    query_raw = jnp.dot(normalized_rows, wq_full, preferred_element_type=f32)
    key_unrotated = jnp.dot(normalized_rows, wk_full, preferred_element_type=f32)
    value_tokens = jnp.dot(normalized_rows, wv_full, preferred_element_type=f32).astype(
        brain_float_half
    )

    def query_path(unrotated_portion, gain_vector):
        return rotary_apply(
            rms_normalize(
                unrotated_portion.reshape(token_rows, QUERY_HEADS, HEAD_SIZE), gain_vector
            ),
            cosine_table,
            sine_table,
        )

    def key_path(unrotated_portion, gain_vector):
        return rotary_apply(
            rms_normalize(
                unrotated_portion.reshape(token_rows, KEY_VALUE_HEADS, HEAD_SIZE), gain_vector
            ),
            cosine_table,
            sine_table,
        )

    query_rotated, query_pull = jax.vjp(query_path, query_raw, query_gain.astype(f32))
    key_rotated, key_pull = jax.vjp(key_path, key_unrotated, key_gain.astype(f32))
    query_outbound = query_rotated.astype(brain_float_half).reshape(
        token_rows, KEY_VALUE_HEADS, group_width * HEAD_SIZE
    )
    key_value_outbound = jnp.concatenate(
        [
            key_rotated.astype(brain_float_half),
            value_tokens.reshape(token_rows, KEY_VALUE_HEADS, HEAD_SIZE),
        ],
        axis=-1,
    )
    query_head_rows, kv_heads = (
        lax.all_to_all(query_outbound, "seq", split_axis=1, concat_axis=0, tiled=True),
        lax.all_to_all(key_value_outbound, "seq", split_axis=1, concat_axis=0, tiled=True),
    )
    group_rows = query_head_rows.shape[0]
    local_heads = query_head_rows.shape[1]
    block_rows = min(512, group_rows)
    count_blocks = group_rows // block_rows
    document_index, _ = doc_table(lengths_row, 0, group_rows)
    key_part = kv_heads[..., :HEAD_SIZE]
    value_part = kv_heads[..., HEAD_SIZE:]
    query_block_list = query_head_rows.reshape(
        count_blocks, block_rows, local_heads, group_width, HEAD_SIZE
    )
    row_table = jnp.arange(group_rows, dtype=jnp.int32).reshape(count_blocks, block_rows)
    doc_blocks = document_index.reshape(count_blocks, block_rows)
    key_spots = jnp.arange(group_rows, dtype=jnp.int32)

    def block_scores(query_block, row_ids, row_docs):
        scores = (
            jnp.einsum("qhgd,khd->hgqk", query_block, key_part, preferred_element_type=f32)
            * score_scale
        )
        allowed = (row_docs[:, None] == document_index[None, :]) & (
            key_spots[None, :] <= row_ids[:, None]
        )
        return jnp.where(allowed[None, None], scores, NEGATIVE)

    def forward_block(block_item):
        query_block, row_ids, row_docs = block_item
        scores = block_scores(query_block, row_ids, row_docs)
        row_max = jnp.max(scores, axis=-1, keepdims=True)
        exp_scores = jnp.exp(scores - row_max)
        row_total = jnp.sum(exp_scores, axis=-1, keepdims=True)
        probability = (exp_scores / row_total).astype(brain_float_half)
        output_rows = jnp.einsum(
            "hgqk,khd->qhgd", probability, value_part, preferred_element_type=f32
        ).astype(brain_float_half)
        return (output_rows, (row_max + jnp.log(row_total))[..., 0])

    attended_blocks, lse_blocks = lax.map(forward_block, (query_block_list, row_table, doc_blocks))
    attended_heads = attended_blocks.reshape(group_rows, local_heads, group_width * HEAD_SIZE)
    attended_tok = lax.all_to_all(
        attended_heads, "seq", split_axis=0, concat_axis=1, tiled=True
    ).reshape(token_rows, QUERY_HEADS * HEAD_SIZE)
    branch = jnp.einsum("tc,dc->td", attended_tok, wo_full, preferred_element_type=f32)
    resid = tok_f32 + branch
    wg_full, wu_full, wd_full, ffn_gain_full = (
        lax.all_gather(gate_weight, "fsdp", axis=0, tiled=True),
        lax.all_gather(up_weight, "fsdp", axis=0, tiled=True),
        lax.all_gather(down_weight, "fsdp", axis=0, tiled=True),
        lax.all_gather(ffn_gain, "fsdp", axis=0, tiled=True),
    )
    normed_two_f32, norm_two_pull = jax.vjp(rms_normalize, resid, ffn_gain_full.astype(f32))
    normed_two = normed_two_f32.astype(brain_float_half)
    gate_pre = jnp.dot(normed_two, wg_full, preferred_element_type=f32)
    up_pre = jnp.dot(normed_two, wu_full, preferred_element_type=f32)

    def swiglu(gate_in, up_in):
        return gate_in * jax.nn.sigmoid(gate_in) * up_in

    hidden_f32, swiglu_pull = jax.vjp(swiglu, gate_pre, up_pre)
    hidden = hidden_f32.astype(brain_float_half)
    down_out = jnp.einsum("tf,df->td", hidden, wd_full, preferred_element_type=f32)
    mixed_own = (resid + down_out).astype(brain_float_half)
    cot_f32 = cot_owned.astype(f32)
    hidden_grad = jnp.dot(cot_owned, wd_full, preferred_element_type=f32)
    gate_grad_f32, up_grad_f32 = swiglu_pull(hidden_grad)
    gate_grad = gate_grad_f32.astype(brain_float_half)
    up_grad = up_grad_f32.astype(brain_float_half)
    normed_two_grad = jnp.einsum(
        "tf,df->td", gate_grad, wg_full, preferred_element_type=f32
    ) + jnp.einsum("tf,df->td", up_grad, wu_full, preferred_element_type=f32)
    resid_part, ffn_gain_part = norm_two_pull(normed_two_grad)
    resid_grad = cot_f32 + resid_part
    branch_grad = resid_grad.astype(brain_float_half)
    attention_output_grad = jnp.dot(branch_grad, wo_full, preferred_element_type=f32).astype(
        brain_float_half
    )
    attended_grad_heads = lax.all_to_all(
        attention_output_grad.reshape(token_rows, KEY_VALUE_HEADS, group_width * HEAD_SIZE),
        "seq",
        split_axis=1,
        concat_axis=0,
        tiled=True,
    )
    grad_blocks = attended_grad_heads.reshape(
        count_blocks, block_rows, local_heads, group_width, HEAD_SIZE
    )

    def backward_block(carry_state, block_item):
        key_accum, value_accum = carry_state
        query_block, grad_block, lse_block, row_ids, row_docs = block_item
        scores = block_scores(query_block, row_ids, row_docs)
        probability = jnp.exp(scores - lse_block[..., None])
        prob_low = probability.astype(brain_float_half)
        value_accum = value_accum + jnp.einsum(
            "hgqk,qhgd->khd", prob_low, grad_block, preferred_element_type=f32
        )
        prob_grad = jnp.einsum("qhgd,khd->hgqk", grad_block, value_part, preferred_element_type=f32)
        inner_sum = jnp.sum(probability * prob_grad, axis=-1, keepdims=True)
        score_grad = (probability * (prob_grad - inner_sum)).astype(brain_float_half)
        query_grad = (
            jnp.einsum("hgqk,khd->qhgd", score_grad, key_part, preferred_element_type=f32)
            * score_scale
        ).astype(brain_float_half)
        key_accum = key_accum + jnp.einsum(
            "hgqk,qhgd->khd", score_grad, query_block, preferred_element_type=f32
        )
        return ((key_accum, value_accum), query_grad)

    zero_state = jnp.zeros((group_rows, local_heads, HEAD_SIZE), f32)
    (key_accum, value_accum), query_grads = lax.scan(
        backward_block,
        (zero_state, zero_state),
        (query_block_list, grad_blocks, lse_blocks, row_table, doc_blocks),
    )
    query_grad_heads = query_grads.reshape(group_rows, local_heads, group_width * HEAD_SIZE)
    kv_grad_heads = jnp.concatenate(
        [(key_accum * score_scale).astype(brain_float_half), value_accum.astype(brain_float_half)],
        axis=-1,
    )
    query_grad_tok, key_value_grad_tokens = (
        lax.all_to_all(query_grad_heads, "seq", split_axis=0, concat_axis=1, tiled=True),
        lax.all_to_all(kv_grad_heads, "seq", split_axis=0, concat_axis=1, tiled=True),
    )
    query_raw_f32, query_gain_part = query_pull(
        query_grad_tok.reshape(token_rows, QUERY_HEADS, HEAD_SIZE).astype(f32)
    )
    key_raw_f32, key_gain_part = key_pull(key_value_grad_tokens[..., :HEAD_SIZE].astype(f32))
    query_raw_grad = query_raw_f32.astype(brain_float_half)
    key_raw_grad = key_raw_f32.astype(brain_float_half)
    value_gradient = key_value_grad_tokens[..., HEAD_SIZE:].reshape(
        token_rows, KEY_VALUE_HEADS * HEAD_SIZE
    )
    normed_grad = (
        jnp.einsum("tc,dc->td", query_raw_grad, wq_full, preferred_element_type=f32)
        + jnp.einsum("tc,dc->td", key_raw_grad, wk_full, preferred_element_type=f32)
        + jnp.einsum("tc,dc->td", value_gradient, wv_full, preferred_element_type=f32)
    )
    tok_part, attn_gain_part = norm_one_pull(normed_grad)
    input_grad_own = (resid_grad + tok_part).astype(brain_float_half)
    column_widths = (
        wq_full.shape[1],
        wk_full.shape[1],
        wv_full.shape[1],
        wo_full.shape[1],
        wg_full.shape[1],
        wu_full.shape[1],
        wd_full.shape[1],
    )
    shard_terms = lax.psum_scatter(
        jnp.concatenate(
            [
                outer_rows(normalized_rows, query_raw_grad),
                outer_rows(normalized_rows, key_raw_grad),
                outer_rows(normalized_rows, value_gradient),
                outer_rows(branch_grad, attended_tok),
                outer_rows(normed_two, gate_grad),
                outer_rows(normed_two, up_grad),
                outer_rows(cot_owned, hidden),
            ],
            axis=1,
        ).astype(jnp.bfloat16),
        "fsdp",
        scatter_dimension=0,
        tiled=True,
    ).astype(jnp.float32)
    shard_terms = lax.psum(shard_terms.astype(jnp.bfloat16), "seq").astype(jnp.float32)
    pieces = split_wide(shard_terms, column_widths)
    gain_totals = lax.psum(
        (attn_gain_part, ffn_gain_part, query_gain_part, key_gain_part), ("fsdp", "seq")
    )
    gain_rows = D // groups
    fsdp_index = lax.axis_index("fsdp")
    attn_gain_grad = lax.dynamic_slice_in_dim(gain_totals[0], fsdp_index * gain_rows, gain_rows, 0)
    ffn_gain_grad = lax.dynamic_slice_in_dim(gain_totals[1], fsdp_index * gain_rows, gain_rows, 0)
    back_mixed, back_grad = (
        lax.all_to_all(mixed_own, "fsdp", split_axis=0, concat_axis=0, tiled=True),
        lax.all_to_all(input_grad_own, "fsdp", split_axis=0, concat_axis=0, tiled=True),
    )
    return (
        back_mixed[send_spot],
        back_grad[send_spot],
        pieces[0],
        pieces[1],
        pieces[2],
        pieces[3],
        pieces[4],
        pieces[5],
        pieces[6],
        attn_gain_grad,
        ffn_gain_grad,
        gain_totals[2],
        gain_totals[3],
    )


def solution(mesh):
    in_specs = (
        P(("fsdp", "seq"), None),
        P(("fsdp", "seq"), None),
        P("fsdp", None),
        P(("fsdp", "seq")),
        P("fsdp", None),
        P("fsdp", None),
        P("fsdp", None),
        P("fsdp", None),
        P("fsdp", None),
        P("fsdp", None),
        P("fsdp", None),
        P("fsdp"),
        P("fsdp"),
        P(),
        P(),
    )
    out_specs = (
        P(("fsdp", "seq"), None),
        P(("fsdp", "seq"), None),
        P("fsdp", None),
        P("fsdp", None),
        P("fsdp", None),
        P("fsdp", None),
        P("fsdp", None),
        P("fsdp", None),
        P("fsdp", None),
        P("fsdp"),
        P("fsdp"),
        P(),
        P(),
    )
    return jax.shard_map(body, mesh=mesh, in_specs=in_specs, out_specs=out_specs, check_vma=False)
```

profile of v0, /device:TPU:0, one launch (start us, length us, event | category | flops | bytes accessed | tf_op | source)
XLA Modules:
  0.0 3398.7 jit_solution(15708500680278727262)
XLA Ops:
  24.4 55.6 %all-gather = bf16[8,1,256]{2,1,0:T(2,128)(2,1)S(1)} all-gather(bf16[1,1,256]{2,1,0:T(2,128)(2,1)S(1)} %reshape.531), channel_id=1, replica_groups=mesh['fsdp'=8,'seq'=4] {'fsdp'}, dimensions={0}, use_global_device_ids=true | all-gather | bytes 4608 | tf_op jit(solution)/shard_map/all_gather | solution.py:108
  122.0 61.8 %all-gather.10.cloned.1.call-done = bf16[2048,2048]{1,0:T(8,128)(2,1)} async-done(((bf16[256,2048]{1,0:T(8,128)(2,1)}), bf16[2048,2048]{1,0:T(8,128)(2,1)}) %all-gather.10.cloned.1.call-update) | async-done | bytes 8388624 | tf_op jit(solution)/shard_map/all_gather | solution.py:104
  240.0 196.7 %while.28 = (s32[]{:T(128)}, bf16[4,512,2,4,64]{1,4,3,2,0:T(8,128)(2,1)}, f32[4,2,4,512]{3,2,1,0:T(4,128)}, s32[4,512]{1,0:T(4,128)S(1)}, s32[2048]{0:T(1024)S(1...) while((s32[]{:T(128)}, ...), condition=%wide.region_10.11_spmd.clone, body=%wide.region_7.10_spmd.clone.sunk | while | flops 2251550720 | bytes 107106424 | solution.py:193
  508.5 91.0 %all-gather.18.cloned.1.call-done = bf16[2048,8192]{1,0:T(8,128)(2,1)} async-done(((bf16[256,8192]{1,0:T(8,128)(2,1)}), bf16[2048,8192]{1,0:T(8,128)(2,1)}) %all-gather.18.cloned.1.call-update) | async-done | bytes 33554448 | tf_op jit(solution)/shard_map/all_gather | solution.py:201
  599.4 26.7 fusion.93
  626.1 261.6 %all-gather.20.cloned.1.call-done = bf16[2048,8192]{1,0:T(8,128)(2,1)} async-done(((bf16[256,8192]{1,0:T(8,128)(2,1)}), bf16[2048,8192]{1,0:T(8,128)(2,1)}) %all-gather.20.cloned.1.call-update) | async-done | bytes 33554448 | tf_op jit(solution)/shard_map/all_gather | solution.py:202
  887.7 26.9 fusion.94
  914.6 261.5 %all-gather.22.cloned.1.call-done = bf16[2048,8192]{1,0:T(8,128)(2,1)} async-done(((bf16[256,8192]{1,0:T(8,128)(2,1)}), bf16[2048,8192]{1,0:T(8,128)(2,1)}) %all-gather.22.cloned.1.call-update) | async-done | bytes 33554448 | tf_op jit(solution)/shard_map/all_gather | solution.py:203
  1176.1 38.4 %multiply_convert_fusion = (bf16[512,8192]{1,0:T(8,128)(2,1)}, bf16[512,8192]{1,0:T(8,128)(2,1)}, bf16[512,8192]{1,0:T(8,128)(2,1)}) fusion(f32[512,8192]{1,0:T(8,128)} %fusion.93, f32[512,8192]{1,0:T(8,128)} %fusion.94, bf16[512,2048]{1,0:T(8,128)(2,1)} %bitcast.27, bf16[2048,8192]{1,0:T(8,128)(2,1)} %all-gather.22.cloned.1.call-done), kind=kOutput, calls=%fused_computation.79 | convolution fusion | flops 17246978048 | bytes 94371840 | tf_op jit(solution)/shard_map/dot_general | solution.py:219
  1214.5 25.4 fusion.95
  1239.9 27.3 multiply_reduce_fusion.1
  1288.0 25.6 all-to-all-done.6
  1319.3 415.0 %while.29 = (s32[]{:T(128)}, f32[2048,2,64]{0,2,1:T(8,128)S(1)}, f32[2048,2,64]{0,2,1:T(8,128)}, bf16[4,512,2,4,64]{1,4,3,2,0:T(8,128)(2,1)}, bf16[4,512,2,4,64]...) while((s32[]{:T(128)}, f32[2048,2,64]{0,2,1:T(8,128)S(1)}, ...), condition=%wide.region_15.16_spmd.clone, body=%wide.region_13.15_spmd.clone.sunk | while | flops 5499252736 | bytes 272765120 | solution.py:265
  1361.0 27.8 fusion.174
  1464.6 27.8 fusion.174
  1568.2 27.8 fusion.174
  1671.8 27.8 fusion.174
  1865.0 25.2 convert_dynamic-update-slice_fusion.2
  1890.2 25.2 convert_dynamic-update-slice_fusion.1
  1939.0 1149.2 %reduce-scatter.4.cloned.1.call-done = bf16[256,29696]{1,0:T(8,128)(2,1)} async-done(((bf16[2048,29696]{1,0:T(8,128)(2,1)}), bf16[256,29696]{1,0:T(8,128)(2,1)}) %reduce-scatter.4.cloned.1.call-update) | async-done | bytes 15204368
  3088.3 25.0 add_convert_fusion
  3132.8 33.5 all-to-all-done.4
  3170.7 69.3 %all-reduce.5 = (f32[2048]{0:T(1024)S(1)}, f32[2048]{0:T(1024)S(1)}, f32[64]{0:T(128)}, f32[64]{0:T(128)}) all-reduce(f32[2048]{0:T(1024)S(1)} %get-tuple-element.205, f32[2048]{0:T(1024)S(1)} %copy-done.64, f32[64]{0:T(128)S(1)} %copy-done.69, f32[64]{0:T(128)S(1)} %copy-done.71), channel_id=1, replica_groups=mesh['fsdp'=8,'seq'=4] {'fsdp','seq'}, use_global_device_ids=true, to_apply=%region_22.23 | all-reduce | flops 4224 | bytes 33792 | tf_op jit(solution)/shard_map/psum | solution.py:323
  3251.7 121.6 %all-reduce.8.cloned.1.call-done = bf16[256,29696]{1,0:T(8,128)(2,1)} async-done(((bf16[256,29696]{1,0:T(8,128)(2,1)}), bf16[256,29696]{1,0:T(8,128)(2,1)}) %all-reduce.8.cloned.1.call-update) | async-done | bytes 15204368 | tf_op jit(solution)/shard_map/psum | solution.py:321
  (373 shorter events, 920.6 us)
Async XLA Ops:
  7.2 95.7 %all-gather.12.cloned.1.call-start = ((), (), s32[]{:S(2)}) async-start(), calls=%async_computation.12 | async-start | bytes 2359296 | tf_op jit(solution)/shard_map/all_gather | solution.py:105
  7.9 105.7 %all-gather.14.cloned.1.call-start = ((), (), s32[]{:S(2)}) async-start(), calls=%async_computation.13 | async-start | bytes 2359296 | tf_op jit(solution)/shard_map/all_gather | solution.py:106
  8.7 175.1 %all-gather.10.cloned.1.call-start = ((), (), s32[]{:S(2)}) async-start(), calls=%async_computation.11 | async-start | bytes 9437184 | tf_op jit(solution)/shard_map/all_gather | solution.py:104
  9.4 488.8 %all-gather.16.cloned.1.call-start = ((), (), s32[]{:S(2)}) async-start(), calls=%async_computation.14 | async-start | bytes 9437184 | tf_op jit(solution)/shard_map/all_gather | solution.py:107
  10.0 589.5 %all-gather.18.cloned.1.call-start = ((), (), s32[]{:S(2)}) async-start(), calls=%async_computation.15 | async-start | bytes 37748736 | tf_op jit(solution)/shard_map/all_gather | solution.py:201
  10.6 877.1 %all-gather.20.cloned.1.call-start = ((), (), s32[]{:S(2)}) async-start(), calls=%async_computation.16 | async-start | bytes 37748736 | tf_op jit(solution)/shard_map/all_gather | solution.py:202
  11.2 1165.0 %all-gather.22.cloned.1.call-start = ((), (), s32[]{:S(2)}) async-start(), calls=%async_computation.17 | async-start | bytes 37748736 | tf_op jit(solution)/shard_map/all_gather | solution.py:203
  17.8 62.3 %copy-start.75 = (bf16[64]{0:T(256)(128)(2,1)S(1)}, bf16[64]{0:T(256)(128)(2,1)}, u32[]{:S(2)}) copy-start(bf16[64]{0:T(256)(128)(2,1)} %param.33) | copy-start | bytes 388
  17.8 84.5 %all-to-all-start = ((bf16[8,64,2048]{2,1,0:T(8,128)(2,1)}), bf16[8,64,2048]{2,1,0:T(8,128)(2,1)S(1)}, u32[]{:S(2)}, u32[]{:S(2)}) async-start(bf16[8,64,2048]{2,1,0:T(8,128)(2,1)} %bitcast.298), calls=%async_computation | async-start | bytes 4194304 | tf_op jit(solution)/shard_map/all_to_all | solution.py:100
  80.1 123.8 %copy-start.65 = (f32[64]{0:T(128)}, f32[64]{0:T(128)S(1)}, u32[]{:S(2)}) copy-start(f32[64]{0:T(128)S(1)} %convert_element_type.153) | copy-start | bytes 772
  80.5 124.9 %copy-start.34 = (f32[512,32]{0,1:T(8,128)}, f32[512,32]{0,1:T(8,128)S(1)}, u32[]{:S(2)}) copy-start(f32[512,32]{0,1:T(8,128)S(1)} %get-tuple-element.287) | copy-start | bytes 196612
  80.5 124.9 %copy-start.36 = (f32[512,32]{0,1:T(8,128)}, f32[512,32]{0,1:T(8,128)S(1)}, u32[]{:S(2)}) copy-start(f32[512,32]{0,1:T(8,128)S(1)} %get-tuple-element.288) | copy-start | bytes 196612
  118.3 90.1 %all-to-all-start.2 = ((bf16[512,8,128]{0,2,1:T(8,128)(2,1)}), bf16[512,8,128]{0,2,1:T(8,128)(2,1)S(1)}, u32[]{:S(2)}, u32[]{:S(2)}) async-start(bf16[512,8,128]{0,2,1:T(8,128)(2,1)} %pad_maximum_fusion.1), calls=%async_computation.2 | async-start | bytes 2097152 | tf_op jit(solution)/shard_map/all_to_all | solution.py:155
  208.4 30.1 all-to-all-start.1
  453.6 29.3 all-to-all-start.3
  482.8 431.8 %all-to-all-start.5 = ((bf16[8,64,2048]{2,1,0:T(8,128)(2,1)}), bf16[8,64,2048]{2,1,0:T(8,128)(2,1)}, u32[]{:S(2)}, u32[]{:S(2)}) async-start(bf16[8,64,2048]{2,1,0:T(8,128)(2,1)} %bitcast.299), calls=%async_computation.5 | async-start | bytes 4194304 | tf_op jit(solution)/shard_map/all_to_all | solution.py:101
  508.4 379.3 %copy-start.22 = (bf16[512,2048]{1,0:T(8,128)(2,1)}, bf16[512,2048]{1,0:T(8,128)(2,1)S(1)}, u32[]{:S(2)}) copy-start(bf16[512,2048]{1,0:T(8,128)(2,1)S(1)} %multiply_convert_fusion.2) | copy-start | bytes 6291460
  1283.5 30.1 all-to-all-start.6
  1737.8 39.5 %all-to-all-start.8 = ((bf16[2048,2,128]{2,1,0:T(2,128)(2,1)}), bf16[2048,2,128]{2,1,0:T(2,128)(2,1)S(1)}, u32[]{:S(2)}, u32[]{:S(2)}) async-start(bf16[2048,2,128]{2,1,0:T(2,128)(2,1)} %copy.125), calls=%async_computation.8 | async-start | bytes 2097152 | tf_op jit(solution)/shard_map/all_to_all | solution.py:277
  1777.3 29.4 all-to-all-start.7
  1781.9 1306.3 %reduce-scatter.4.cloned.1.call-start = ((), (), s32[]{:S(2)}) async-start(), calls=%async_computation.19 | async-start | bytes 136839168
  1939.0 1434.4 %all-reduce.8.cloned.1.call-start = ((), (), s32[]{:S(2)}) async-start(), calls=%async_computation.18 | async-start | bytes 30408704 | tf_op jit(solution)/shard_map/psum | solution.py:321
  3113.3 53.0 %all-to-all-start.4 = ((bf16[8,64,2048]{2,1,0:T(8,128)(2,1)}), bf16[8,64,2048]{2,1,0:T(8,128)(2,1)S(1)}, u32[]{:S(2)}, u32[]{:S(2)}) async-start(bf16[8,64,2048]{2,1,0:T(8,128)(2,1)} %bitcast.320), calls=%async_computation.4 | async-start | bytes 4194304 | tf_op jit(solution)/shard_map/all_to_all | solution.py:331
  3166.3 78.3 %all-to-all-start.9 = ((bf16[8,64,2048]{2,1,0:T(8,128)(2,1)}), bf16[8,64,2048]{2,1,0:T(8,128)(2,1)}, u32[]{:S(2)}, u32[]{:S(2)}) async-start(bf16[8,64,2048]{2,1,0:T(8,128)(2,1)} %bitcast.297), calls=%async_computation.9 | async-start | bytes 4194304 | tf_op jit(solution)/shard_map/all_to_all | solution.py:332
  (80 other events, 884.0 us)
Sparse Core Ops, SparseCore 0:
  9.6 44.0 all-gather.11
  55.3 46.5 all-gather.13
  103.6 80.1 all-gather.9
  185.3 80.5 all-gather.15
  267.3 332.0 all-gather.17
  600.9 286.7 all-gather.19
  889.3 286.8 all-gather.21
  1939.1 1149.1 reduce-scatter.3
  3092.2 281.0 all-reduce.7
where the time goes:
time: 3410 us; the launch traced here: 3400 us
  waiting for transfers between devices  2080 us (61%)
  matrix products  730 us (21%)
  other arithmetic  212 us (6%)
  local copies, waits for them, and re-layouts  181 us (5%)
  blocking collectives  133 us (4%)
  starting transfers between devices  48.3 us (1%)
    unnamed x10, waiting for transfers between devices  1150 us
    all_gather x1, waiting for transfers between devices, body(): lax.all_gather(up_weight, 'fsdp', axis=0, tiled=True)  262 us
    all_gather x1, waiting for transfers between devices, body(): lax.all_gather(down_weight, 'fsdp', axis=0, tiled=True)  262 us
    psum x1, waiting for transfers between devices, body(): lax.psum(shard_terms.astype(jnp.bfloat16), 'seq').astype(jnp.float32)  122 us
    dot_general x8, matrix products, block_scores(): jnp.einsum('qhgd,khd->hgqk', query_block, key_part, preferred_element_typ...  115 us
    convert_element_type x4, other arithmetic, backward_block(): (probability * (prob_grad - inner_sum)).astype(brain_float_half)  111 us
    dot_general x4, matrix products, backward_block(): jnp.einsum('qhgd,khd->hgqk', grad_block, value_part, preferred_element_ty...  99.1 us
    dot_general x7, matrix products, outer_rows(): jnp.einsum('tr,tc->rc', left_rows, right_cols, preferred_element_type=jnp...  96.6 us
  transfers between devices with their start and end apart: 19, of which 12 were waited for; matrix products, arithmetic and copies ran while one was open for 13% of the time, Pallas kernels for 0%

commit v1 on v0

v1 whole, which is shorter than its diff:
```python
import functools
import math

import jax
import jax.numpy as jnp
from jax import lax
from jax.experimental import pallas as pl
from jax.experimental.pallas import tpu as pltpu
from jax.sharding import PartitionSpec as P

QUERY_HEADS = 32
KEY_VALUE_HEADS = 8
HEAD_SIZE = 64
HALF = HEAD_SIZE // 2
GROUP_HEADS = QUERY_HEADS // KEY_VALUE_HEADS

EPS = 1e-05
THETA = 1000000.0
SCALE = 1.0 / math.sqrt(HEAD_SIZE)
LOG2E = math.log2(math.e)
F32 = jnp.float32
BF16 = jnp.bfloat16


def dot(left, right, left_dim, right_dim):
    return lax.dot_general(
        left, right, (((left_dim,), (right_dim,)), ((), ())), preferred_element_type=F32
    )


def rms_rope(raw, gain, cosine, sine):
    normed = raw * lax.rsqrt(jnp.mean(raw * raw, axis=0, keepdims=True) + EPS) * gain
    first, second = normed[:HALF], normed[HALF:]
    return jnp.concatenate(
        [first * cosine - second * sine, second * cosine + first * sine], axis=0
    )


def rms_rope_back(raw, gain, cosine, sine, grad):
    first, second = grad[:HALF], grad[HALF:]
    turned = jnp.concatenate(
        [first * cosine + second * sine, second * cosine - first * sine], axis=0
    )
    scale = lax.rsqrt(jnp.mean(raw * raw, axis=0, keepdims=True) + EPS)
    unit = raw * scale
    weighted = gain * turned
    raw_grad = scale * (weighted - unit * jnp.mean(weighted * unit, axis=0, keepdims=True))
    return raw_grad, turned * unit


def attend_kernel(
    block, low_ref, order_ref, q_raw, k_raw, v_raw, start_ref, cos_ref, sin_ref, gains_ref,
    out_ref, q_out, k_out, v_out, lse_ref, k_rows, acc, total,
):
    step = pl.program_id(1)
    query_gain, key_gain = gains_ref[0], gains_ref[1]

    @pl.when(step == 0)
    def _():
        token_rows = k_raw.shape[2]
        for r in range(k_raw.shape[0]):
            part = slice(r * token_rows, (r + 1) * token_rows)
            at = order_ref[r]
            key = rms_rope(k_raw[at], key_gain, cos_ref[:, part], sin_ref[:, part])
            k_out[:, part] = key.astype(BF16)
            k_rows[part, :] = key.T.astype(BF16)
            v_out[:, part] = v_raw[at].astype(BF16)

    columns = pl.ds(pl.multiple_of(step * block, block), block)
    cosine, sine = cos_ref[:, columns], sin_ref[:, columns]
    for g in range(GROUP_HEADS):
        rows = slice(g * HEAD_SIZE, (g + 1) * HEAD_SIZE)
        q_out[rows, :] = rms_rope(q_raw[0, rows, :], query_gain, cosine, sine).astype(BF16)
    acc[...] = jnp.zeros_like(acc)
    total[...] = jnp.zeros_like(total)
    starts = start_ref[...]
    spots = step * block + lax.broadcasted_iota(jnp.int32, (1, block), 1)

    def inner(j, carry):
        keys = pl.ds(pl.multiple_of(j * block, block), block)
        key_rows = k_rows[keys, :]
        value = v_out[:, keys]
        key_spots = j * block + lax.broadcasted_iota(jnp.int32, (block, 1), 0)
        allowed = (key_spots >= starts) & (key_spots <= spots)
        for g in range(GROUP_HEADS):
            rows = slice(g * HEAD_SIZE, (g + 1) * HEAD_SIZE)
            score = dot(key_rows, q_out[rows, :], 1, 0)
            prob = jnp.where(allowed, jnp.exp2(score * (SCALE * LOG2E)), 0.0)
            total[g : g + 1, :] += jnp.sum(prob, axis=0, keepdims=True)
            acc[rows, :] += dot(value, prob.astype(BF16), 1, 0)
        return carry

    lax.fori_loop(low_ref[step], step + 1, inner, 0)
    for g in range(GROUP_HEADS):
        rows = slice(g * HEAD_SIZE, (g + 1) * HEAD_SIZE)
        summed = total[g : g + 1, :]
        out_ref[0, rows, :] = (acc[rows, :] / summed).astype(BF16)
        lse_ref[0, g : g + 1, :] = jnp.log2(summed)


def attend_back_kernel(
    block, spans, low_ref, order_ref, q_raw, k_raw, start_ref, cos_ref, sin_ref, gains_ref,
    q_ref, k_ref, v_ref, lse_ref, out_ref, grad_ref,
    d_ref, gain_out, k_rows, v_rows, dq, dk, dv, gain_acc,
):
    head, step = pl.program_id(0), pl.program_id(1)
    steps = pl.num_programs(1)
    local = pl.num_programs(0)
    query_gain, key_gain = gains_ref[0], gains_ref[1]
    width = GROUP_HEADS * HEAD_SIZE
    token_rows = spans * block

    @pl.when((head == 0) & (step == 0))
    def _():
        gain_acc[...] = jnp.zeros_like(gain_acc)
        gain_out[...] = jnp.zeros_like(gain_out)

    @pl.when(step == 0)
    def _():
        k_rows[...] = k_ref[...].astype(F32).T.astype(BF16)
        v_rows[...] = v_ref[...].astype(F32).T.astype(BF16)
        dk[...] = jnp.zeros_like(dk)
        dv[...] = jnp.zeros_like(dv)

    columns = pl.ds(pl.multiple_of(step * block, block), block)
    cosine, sine = cos_ref[:, columns], sin_ref[:, columns]
    dq[...] = jnp.zeros_like(dq)
    starts = start_ref[...]
    spots = step * block + lax.broadcasted_iota(jnp.int32, (1, block), 1)
    inner_sums = [
        jnp.sum(
            out_ref[0, g * HEAD_SIZE : (g + 1) * HEAD_SIZE, :].astype(F32)
            * grad_ref[0, g * HEAD_SIZE : (g + 1) * HEAD_SIZE, :].astype(F32),
            axis=0,
            keepdims=True,
        )
        for g in range(GROUP_HEADS)
    ]

    def inner(j, carry):
        keys = pl.ds(pl.multiple_of(j * block, block), block)
        key_rows, value_rows, key = k_rows[keys, :], v_rows[keys, :], k_ref[:, keys]
        key_spots = j * block + lax.broadcasted_iota(jnp.int32, (block, 1), 0)
        allowed = (key_spots >= starts) & (key_spots <= spots)
        key_sum = jnp.zeros((HEAD_SIZE, block), F32)
        value_sum = jnp.zeros((HEAD_SIZE, block), F32)
        for g in range(GROUP_HEADS):
            rows = slice(g * HEAD_SIZE, (g + 1) * HEAD_SIZE)
            query, grad = q_ref[rows, :], grad_ref[0, rows, :]
            score = dot(key_rows, query, 1, 0) * (SCALE * LOG2E) - lse_ref[0, g : g + 1, :]
            prob = jnp.where(allowed, jnp.exp2(score), 0.0)
            prob_grad = dot(value_rows, grad, 1, 0)
            score_grad = (prob * (prob_grad - inner_sums[g])).astype(BF16)
            value_sum += dot(grad, prob.astype(BF16), 1, 1)
            key_sum += dot(query, score_grad, 1, 1)
            dq[rows, :] += dot(key, score_grad, 1, 0)
        dk[:, keys] += key_sum
        dv[:, keys] += value_sum
        return carry

    lax.fori_loop(low_ref[step], step + 1, inner, 0)
    span = step // spans
    inside = pl.ds(pl.multiple_of((step % spans) * block, block), block)
    for g in range(GROUP_HEADS):
        rows = slice(g * HEAD_SIZE, (g + 1) * HEAD_SIZE)
        grad = (dq[rows, :] * SCALE).astype(BF16).astype(F32)
        raw_grad, terms = rms_rope_back(q_raw[0, rows, :], query_gain, cosine, sine, grad)
        d_ref[order_ref[span], pl.ds(pl.multiple_of(head * width + g * HEAD_SIZE, HEAD_SIZE), HEAD_SIZE), inside] = (
            raw_grad.astype(BF16)
        )
        gain_acc[...] += terms

    @pl.when(step == steps - 1)
    def _():
        key_at = pl.ds(pl.multiple_of(local * width + head * HEAD_SIZE, HEAD_SIZE), HEAD_SIZE)
        value_at = pl.ds(
            pl.multiple_of(local * (width + HEAD_SIZE) + head * HEAD_SIZE, HEAD_SIZE), HEAD_SIZE
        )
        for r in range(d_ref.shape[0]):
            part = slice(r * token_rows, (r + 1) * token_rows)
            grad = (dk[:, part] * SCALE).astype(BF16).astype(F32)
            raw_grad, terms = rms_rope_back(
                k_raw[order_ref[r]], key_gain, cos_ref[:, part], sin_ref[:, part], grad
            )
            d_ref[order_ref[r], key_at, :] = raw_grad.astype(BF16)
            d_ref[order_ref[r], value_at, :] = dv[:, part].astype(BF16)
            gain_out[1] += jnp.broadcast_to(
                jnp.sum(terms, axis=1, keepdims=True), gain_out.shape[1:]
            )

    @pl.when((step == steps - 1) & (head == local - 1))
    def _():
        gain_out[0] = jnp.broadcast_to(
            jnp.sum(gain_acc[...], axis=1, keepdims=True), gain_out.shape[1:]
        )


def attention_specs(block, group_rows, local, spans):
    width = GROUP_HEADS * HEAD_SIZE
    tables = [
        pl.BlockSpec((1, block), lambda h, s, low, order: (0, s)),
        pl.BlockSpec((HALF, group_rows), lambda h, s, low, order: (0, 0)),
        pl.BlockSpec((HALF, group_rows), lambda h, s, low, order: (0, 0)),
        pl.BlockSpec((2, HEAD_SIZE, 1), lambda h, s, low, order: (0, 0, 0)),
    ]
    q_block = pl.BlockSpec((width, block), lambda h, s, low, order: (h, s))
    k_block = pl.BlockSpec((HEAD_SIZE, group_rows), lambda h, s, low, order: (h, 0))
    raw_q = pl.BlockSpec(
        (1, width, block), lambda h, s, low, order: (order[s // spans], h, s % spans)
    )
    ranks, token_rows = group_rows // (spans * block), spans * block
    raw_k = pl.BlockSpec(
        (ranks, HEAD_SIZE, token_rows),
        lambda h, s, low, order: (0, local * GROUP_HEADS + h, 0),
    )
    raw_v = pl.BlockSpec(
        (ranks, HEAD_SIZE, token_rows),
        lambda h, s, low, order: (0, local * (GROUP_HEADS + 1) + h, 0),
    )
    lse = pl.BlockSpec((1, 8, block), lambda h, s, low, order: (h, 0, s))
    return tables, q_block, k_block, raw_q, raw_k, raw_v, lse


def attend(qkv_raw, low, order, starts, cosine, sine, gains, ranks, local, block):
    token_rows = qkv_raw.shape[2]
    group_rows = token_rows * ranks
    spans = token_rows // block
    width = GROUP_HEADS * HEAD_SIZE
    tables, q_block, k_block, raw_q, raw_k, raw_v, lse = attention_specs(
        block, group_rows, local, spans
    )
    return pl.pallas_call(
        functools.partial(attend_kernel, block),
        out_shape=(
            jax.ShapeDtypeStruct((ranks, local * width, token_rows), BF16),
            jax.ShapeDtypeStruct((local * width, group_rows), BF16),
            jax.ShapeDtypeStruct((local * HEAD_SIZE, group_rows), BF16),
            jax.ShapeDtypeStruct((local * HEAD_SIZE, group_rows), BF16),
            jax.ShapeDtypeStruct((local, 8, group_rows), F32),
        ),
        grid_spec=pltpu.PrefetchScalarGridSpec(
            num_scalar_prefetch=2,
            grid=(local, group_rows // block),
            in_specs=[raw_q, raw_k, raw_v, *tables],
            out_specs=[raw_q, q_block, k_block, k_block, lse],
            scratch_shapes=[
                pltpu.VMEM((group_rows, HEAD_SIZE), BF16),
                pltpu.VMEM((width, block), F32),
                pltpu.VMEM((8, block), F32),
            ],
        ),
        compiler_params=pltpu.CompilerParams(vmem_limit_bytes=40 << 20),
        cost_estimate=pl.CostEstimate(
            flops=20 * local * width * group_rows * group_rows,
            bytes_accessed=12 * local * width * group_rows,
            transcendentals=local * GROUP_HEADS * group_rows * group_rows,
        ),
        name="attend",
    )(low, order, qkv_raw, qkv_raw, qkv_raw, starts, cosine, sine, gains)


def attend_back(
    qkv_raw, low, order, starts, cosine, sine, gains, query, key, value, lse_table, attended, grad,
    ranks, local, block,
):
    token_rows = qkv_raw.shape[2]
    group_rows = token_rows * ranks
    spans = token_rows // block
    width = GROUP_HEADS * HEAD_SIZE
    total = local * (width + 2 * HEAD_SIZE)
    tables, q_block, k_block, raw_q, raw_k, _, lse = attention_specs(
        block, group_rows, local, spans
    )
    return pl.pallas_call(
        functools.partial(attend_back_kernel, block, spans),
        out_shape=(
            jax.ShapeDtypeStruct((ranks, total, token_rows), BF16),
            jax.ShapeDtypeStruct((2, HEAD_SIZE, 128), F32),
        ),
        grid_spec=pltpu.PrefetchScalarGridSpec(
            num_scalar_prefetch=2,
            grid=(local, group_rows // block),
            in_specs=[
                raw_q, raw_k, *tables, q_block, k_block, k_block, lse, raw_q, raw_q,
            ],
            out_specs=[
                pl.BlockSpec((ranks, total, token_rows), lambda h, s, low, order: (0, 0, 0)),
                pl.BlockSpec((2, HEAD_SIZE, 128), lambda h, s, low, order: (0, 0, 0)),
            ],
            scratch_shapes=[
                pltpu.VMEM((group_rows, HEAD_SIZE), BF16),
                pltpu.VMEM((group_rows, HEAD_SIZE), BF16),
                pltpu.VMEM((width, block), F32),
                pltpu.VMEM((HEAD_SIZE, group_rows), F32),
                pltpu.VMEM((HEAD_SIZE, group_rows), F32),
                pltpu.VMEM((HEAD_SIZE, block), F32),
            ],
        ),
        compiler_params=pltpu.CompilerParams(vmem_limit_bytes=48 << 20),
        cost_estimate=pl.CostEstimate(
            flops=27 * local * width * group_rows * group_rows,
            bytes_accessed=16 * local * width * group_rows,
            transcendentals=local * GROUP_HEADS * group_rows * group_rows,
        ),
        name="attend_back",
    )(
        low, order, qkv_raw, qkv_raw, starts, cosine, sine, gains, query, key, value, lse_table,
        attended, grad,
    )


def rms_parts(rows, gain):
    scale = lax.rsqrt(jnp.mean(rows * rows, axis=-1, keepdims=True) + EPS)
    return scale, (rows * scale * gain).astype(BF16)


def rms_back(rows, scale, gain, grad):
    unit = rows * scale
    weighted = grad * gain
    row_grad = scale * (weighted - unit * jnp.mean(weighted * unit, axis=-1, keepdims=True))
    return row_grad, jnp.sum(grad * unit, axis=0)


def hop(rows, distance, ranks):
    return lax.ppermute(rows, "seq", [(i, i ^ distance) for i in range(ranks)])


def after(values, *first):
    return lax.optimization_barrier((values, first))[0]


def gather_chunks(rows, ranks):
    half = rows.shape[0] // 2
    if ranks != 4:
        moved = [rows] + [hop(rows, k, ranks) for k in range(1, ranks)]
        return [(m[:half], m[half:]) for m in moved]
    first, second = hop(rows, 1, ranks), hop(rows, 2, ranks)
    corner = hop(first[:half], 2, ranks), hop(second[half:], 1, ranks)
    return [(m[:half], m[half:]) for m in (rows, first, second)] + [corner]


def scatter_chunks(make, given, ranks, early=((), None), late=((), None)):
    def run(work, arrays):
        return work[1](arrays) if work[1] else ()

    if ranks != 4:
        sent = [make(k, given) for k in range(1, ranks)]
        sent, first, second = lax.optimization_barrier((sent, early[0], late[0]))
        own = make(0, given)
        more = run(early, first), run(late, second)
        moved = [hop(part, k + 1, ranks) for k, part in enumerate(sent)]
        moved, own, more = lax.optimization_barrier((moved, own, more))
        return sum((m.astype(F32) for m in moved), own.astype(F32)), *more
    corner = make(3, given)
    half = corner.shape[0] // 2
    corner, given, arrays = lax.optimization_barrier((corner, given, early[0]))
    for_second = hop(corner[:half], 1, ranks)
    for_first = hop(corner[half:], 2, ranks)
    first, second, early = make(1, given), make(2, given), run(early, arrays)

    def add(a, b):
        return (a.astype(F32) + b.astype(F32)).astype(BF16)

    first = jnp.concatenate([first[:half], add(first[half:], for_first)])
    second = jnp.concatenate([add(second[:half], for_second), second[half:]])
    first, second, given, early, arrays = lax.optimization_barrier(
        (first, second, given, early, late[0])
    )
    own, late = make(0, given), run(late, arrays)
    first, second, own, late = lax.optimization_barrier(
        (hop(first, 1, ranks), hop(second, 2, ranks), own, late)
    )
    return own.astype(F32) + first.astype(F32) + second.astype(F32), early, late


def up_kernel(tile, xa, xb, w_ref, *rest):
    f_ref, hid_ref, x_ref, x_all = rest[-4:]
    half = xa.shape[0]

    @pl.when(pl.program_id(0) == 0)
    def _():
        x_all[:half, :] = xa[...]
        x_all[half:, :] = xb[...]
        x_ref[...] = x_all[...]

    for i in range(w_ref.shape[1] // (2 * tile)):
        left, right = 2 * i * tile, (2 * i + 1) * tile
        both = dot(x_all[...], w_ref[:, left : left + 2 * tile], 1, 0)
        gate, up = both[:, :tile], both[:, tile:]
        gated = jax.nn.sigmoid(gate)
        silu = gate * gated
        hid_ref[:, i * tile : (i + 1) * tile] = (silu * up).astype(BF16)
        f_ref[:, left:right] = up * (gated + silu * (1.0 - gated))
        f_ref[:, right : right + tile] = silu


def up_chunk(k, x, gate_up, before, ranks, tile):
    half, features = x[0].shape
    rows, width = 2 * half, gate_up.shape[1]
    halves = [pl.BlockSpec((half, features), lambda t: (0, 0))] * 2
    step = min(2 * tile, width // 2)
    kept = [] if before is None else list(before)
    return pl.pallas_call(
        functools.partial(up_kernel, tile),
        out_shape=(
            jax.ShapeDtypeStruct((ranks * rows, width), F32),
            jax.ShapeDtypeStruct((ranks * rows, width // 2), BF16),
            jax.ShapeDtypeStruct((ranks * rows, features), BF16),
        ),
        grid=(width // (2 * step),),
        in_specs=halves
        + [pl.BlockSpec((features, 2 * step), lambda t: (0, t))]
        + [pl.BlockSpec(memory_space=pl.ANY)] * len(kept),
        out_specs=(
            pl.BlockSpec((rows, 2 * step), lambda t: (k, t)),
            pl.BlockSpec((rows, step), lambda t: (k, t)),
            pl.BlockSpec((rows, features), lambda t: (k, 0)),
        ),
        scratch_shapes=[pltpu.VMEM((rows, features), BF16)],
        input_output_aliases={3 + i: i for i in range(len(kept))},
        compiler_params=pltpu.CompilerParams(vmem_limit_bytes=48 << 20),
        cost_estimate=pl.CostEstimate(
            flops=3 * rows * features * width,
            bytes_accessed=2 * features * width + 5 * rows * width + 4 * rows * features,
            transcendentals=rows * width // 2,
        ),
        name="up_chunk",
    )(*x, gate_up, *kept)


def hidden_back_kernel(tile, c_ref, w_ref, f_ref, d_ref):
    for i in range(w_ref.shape[1] // tile):
        left, right = 2 * i * tile, (2 * i + 1) * tile
        hidden_grad = dot(c_ref[...], w_ref[:, i * tile : (i + 1) * tile], 1, 0)
        d_ref[:, left:right] = (hidden_grad * f_ref[:, left:right]).astype(BF16)
        d_ref[:, right : right + tile] = (hidden_grad * f_ref[:, right : right + tile]).astype(BF16)


def hidden_back(cot, down, factors, tile, rows):
    group_rows, features = cot.shape
    width = down.shape[1]
    step = min(2 * tile, width)
    return pl.pallas_call(
        functools.partial(hidden_back_kernel, tile),
        out_shape=jax.ShapeDtypeStruct((group_rows, 2 * width), BF16),
        grid=(group_rows // rows, width // step),
        in_specs=[
            pl.BlockSpec((rows, features), lambda r, t: (r, 0)),
            pl.BlockSpec((features, step), lambda r, t: (0, t)),
            pl.BlockSpec((rows, 2 * step), lambda r, t: (r, t)),
        ],
        out_specs=pl.BlockSpec((rows, 2 * step), lambda r, t: (r, t)),
        compiler_params=pltpu.CompilerParams(vmem_limit_bytes=48 << 20),
        cost_estimate=pl.CostEstimate(
            flops=3 * group_rows * features * width,
            bytes_accessed=4 * features * width + 12 * group_rows * width,
            transcendentals=group_rows * width,
        ),
        name="hidden_back",
    )(cot, down, factors)


def widen(pieces, place, columns, part, total, ranks):
    rows = 2 * pieces[0][0][0].shape[0]
    each = sum(stop - start for start, stop in columns)
    width = each * len(pieces)
    if ranks != 4:

        def picked(chunk):
            return jnp.concatenate([chunk[:, a:b] for a, b in columns], axis=1)

        stacked = jnp.stack(
            [
                jnp.concatenate(
                    [jnp.concatenate([picked(p) for p in group[k]]) for group in pieces], axis=1
                )
                for k in range(ranks)
            ]
        )
        ordered = jnp.swapaxes(jnp.take(stacked, place, axis=0), 0, 1)
        return ordered.reshape(rows, ranks * width).astype(F32)
    half = rows // 2
    flat = [p for group in pieces for chunk in group for p in chunk]
    counts = len(pieces)
    whole = pl.BlockSpec((half, part), lambda k, place: (0, total))

    def kernel(place_ref, *refs):
        out = refs[-1]
        for k in range(ranks):

            @pl.when(pl.program_id(0) == k)
            def _(k=k):
                at = 0
                for group in range(counts):
                    for start, stop in columns:
                        for side in range(2):
                            source = refs[(group * ranks + k) * 2 + side]
                            out[side * half : (side + 1) * half, at : at + stop - start] = source[
                                :, start:stop
                            ].astype(F32)
                        at += stop - start

    return pl.pallas_call(
        kernel,
        out_shape=jax.ShapeDtypeStruct((rows, ranks * width), F32),
        grid_spec=pltpu.PrefetchScalarGridSpec(
            num_scalar_prefetch=1,
            grid=(ranks,),
            in_specs=[whole] * len(flat),
            out_specs=pl.BlockSpec((rows, width), lambda k, place: (0, place[k])),
        ),
        compiler_params=pltpu.CompilerParams(vmem_limit_bytes=48 << 20),
        cost_estimate=pl.CostEstimate(
            flops=rows * width * ranks, bytes_accessed=6 * rows * width * ranks, transcendentals=0
        ),
        name="widen",
    )(place, *flat)


def body(
    tokens, mixed_cotangent, lengths, owner_slot, q_weight, key_projection, value_projection,
    out_weight, gate_weight, up_weight, down_weight, attn_gain, ffn_gain, query_gain, key_gain,
):
    groups = lax.axis_size("fsdp")
    ranks = lax.axis_size("seq")
    seq_index = lax.axis_index("seq")
    token_rows, features = tokens.shape
    slice_rows = token_rows // groups
    group_rows = token_rows * ranks
    local = KEY_VALUE_HEADS // ranks
    q_part = q_weight.shape[1] // ranks
    k_part = key_projection.shape[1] // ranks
    f_part = gate_weight.shape[1] // ranks
    h_part = q_part + 2 * k_part
    block = min(256, token_rows)
    tile = min(256, f_part)
    gain_rows = attn_gain.shape[0]

    local_slot = owner_slot % token_rows
    target = owner_slot // token_rows // ranks
    send_spot = target * slice_rows + local_slot % slice_rows
    inverse = (
        jnp.zeros((token_rows,), jnp.int32)
        .at[send_spot]
        .set(jnp.arange(token_rows, dtype=jnp.int32))
    )

    def exchange(rows):
        return lax.all_to_all(rows, "fsdp", split_axis=0, concat_axis=0, tiled=True)

    both_gains = jnp.concatenate([attn_gain, ffn_gain])
    gains_full = exchange(jnp.broadcast_to(both_gains, (groups, 2 * gain_rows))).astype(F32)
    attn_full = gains_full[:, :gain_rows].reshape(features)
    ffn_full = gains_full[:, gain_rows:].reshape(features)
    owned = exchange(tokens[inverse])

    def columns(weight, width):
        return lax.dynamic_slice_in_dim(weight, seq_index * width, width, 1)

    def gather(weight):
        return lax.all_gather(weight, "fsdp", axis=0, tiled=True)

    head_shard = (
        jnp.concatenate(
            [
                columns(q_weight, q_part),
                columns(key_projection, k_part),
                columns(value_projection, k_part),
                columns(out_weight, q_part),
            ],
            axis=1,
        )
    )

    def tiles(weight):
        return columns(weight, f_part).reshape(-1, f_part // tile, tile)

    gate_up_shard = jnp.concatenate([tiles(gate_weight), tiles(up_weight)], axis=2)
    owned, cot_rows, head_shard, gate_up_shard, down_shard = lax.optimization_barrier(
        (
            owned,
            mixed_cotangent[inverse],
            head_shard,
            gate_up_shard.reshape(-1, 2 * f_part),
            columns(down_weight, f_part),
        )
    )
    head_own = gather(head_shard)
    qkv_own, wo_own = head_own[:, :h_part], head_own[:, h_part:]
    gate_up_own = gather(gate_up_shard)
    down_own = gather(down_shard)
    cot_owned = exchange(cot_rows)

    lengths_row = lengths[0]
    token_spots = jnp.arange(group_rows, dtype=jnp.int32)
    seq_ends = jnp.cumsum(lengths_row)
    passed = token_spots[:, None] >= seq_ends[None, :]
    starts = jnp.sum(jnp.where(passed, lengths_row[None, :], 0), axis=1).astype(jnp.int32)
    places = (token_spots - starts).astype(F32)
    freqs = jnp.exp(jnp.arange(HALF, dtype=F32) * (-2.0 * math.log(THETA) / HEAD_SIZE))
    angles = freqs[:, None] * places[None, :]
    cosine, sine = jnp.cos(angles), jnp.sin(angles)
    low = starts[::block] // block
    start_row = starts[None, :]
    head_gains = jnp.stack([query_gain, key_gain]).astype(F32)[:, :, None]
    place = jnp.bitwise_xor(seq_index, jnp.arange(ranks, dtype=jnp.int32)).astype(jnp.int32)

    def together(chunks):
        return jnp.stack([jnp.concatenate(pair) for pair in chunks])

    tok_f32 = owned.astype(F32)
    scale_one, normed_own = rms_parts(tok_f32, attn_full)
    normed = gather_chunks(normed_own, ranks)
    normed[-1], cot_sent = lax.optimization_barrier((normed[-1], cot_owned))
    cot = gather_chunks(cot_sent, ranks)
    normed = together(normed)
    qkv_raw = jnp.stack([dot(qkv_own, normed[k], 0, 1) for k in range(ranks)])
    attended, query, key, value, lse_table = attend(
        qkv_raw, low, place, start_row, cosine, sine, head_gains, ranks, local, block
    )
    branch_sum, cot, _ = scatter_chunks(
        lambda k, given: dot(given[0][k], given[1], 0, 1).astype(BF16),
        (after(attended, cot[:3]), wo_own),
        ranks,
        early=(cot, together),
    )
    resid = tok_f32 + branch_sum

    scale_two, normed_two_own = rms_parts(resid, ffn_full)
    results = None
    for k, chunk in enumerate(gather_chunks(normed_two_own, ranks)):
        results = up_chunk(k, chunk, gate_up_own, results, ranks, tile)
    factors, hidden, normed_two = results
    cot = cot.reshape(group_rows, features)
    gate_up_grad = hidden_back(cot, down_own, factors, tile, token_rows)

    def rows_of(array, k):
        return array[k * token_rows : (k + 1) * token_rows]

    def scatter(terms):
        return lax.psum_scatter(
            terms.astype(BF16), "fsdp", scatter_dimension=0, tiled=True
        )

    def terms_of(left, right):
        return dot(left, right, 0, 0).astype(BF16)

    down_terms = terms_of(cot, hidden)
    normed_two_grad, _, left_terms = scatter_chunks(
        lambda k, given: dot(rows_of(given[0], k), given[1], 1, 1).astype(BF16),
        (gate_up_grad, gate_up_own),
        ranks,
        late=(normed_two, lambda rows: terms_of(rows, gate_up_grad[:, :f_part])),
    )
    down_grad = scatter(down_terms)
    left_grad = scatter(left_terms)
    resid_part, ffn_gain_part = rms_back(resid, scale_two, ffn_full, normed_two_grad)
    resid_grad = cot_owned.astype(F32) + resid_part
    branch_own = resid_grad.astype(BF16)
    branch_own, right_in, hidden = lax.optimization_barrier((branch_own, normed_two, hidden))
    branch = gather_chunks(branch_own, ranks)
    right_terms = terms_of(right_in, gate_up_grad[:, f_part:])
    down_parts = jnp.stack(
        [
            dot(
                lax.dynamic_slice_in_dim(hidden, place[j] * token_rows, token_rows, 0),
                down_own, 1, 1,
            ).astype(BF16)
            for j in range(ranks)
        ]
    )
    branch[-1], right_terms, down_parts = lax.optimization_barrier(
        (branch[-1], right_terms, down_parts)
    )
    branch = together(branch)
    right_grad = scatter(right_terms)
    attended_grad = jnp.stack(
        [dot(wo_own, branch[k], 0, 1).astype(BF16) for k in range(ranks)]
    )
    d_heads, head_gain_parts = attend_back(
        qkv_raw, low, place, start_row, cosine, sine, head_gains, query, key, value, lse_table,
        attended, after(attended_grad, down_grad), ranks, local, block,
    )
    down_moved = lax.all_to_all(down_parts, "seq", split_axis=0, concat_axis=0, tiled=True)
    d_heads = after(d_heads, left_grad)

    def outer(left, right):
        return lax.dot_general(
            left.reshape(ranks, token_rows, features), right,
            (((0, 1), (0, 2)), ((), ())), preferred_element_type=F32,
        ).astype(BF16)

    normed_grad, head_terms, mixed_own = scatter_chunks(
        lambda k, given: dot(given[0][k], given[1], 0, 1).astype(BF16),
        (d_heads, qkv_own),
        ranks,
        early=(
            (d_heads, attended),
            lambda a: jnp.concatenate([outer(normed, a[0]), outer(branch, a[1])], axis=1),
        ),
        late=(down_moved, lambda a: (resid + jnp.sum(a.astype(F32), axis=0)).astype(BF16)),
    )
    head_grad = scatter(head_terms)
    back_mixed = exchange(mixed_own)
    tok_part, attn_gain_part = rms_back(tok_f32, scale_one, attn_full, normed_grad)
    input_grad_own = after((resid_grad + tok_part).astype(BF16), right_grad, back_mixed)
    back_grad = exchange(input_grad_own)

    down_all = gather_chunks(down_grad, ranks)
    left_all = gather_chunks(left_grad, ranks)
    right_all = gather_chunks(right_grad, ranks)
    head_all = gather_chunks(head_grad, ranks)

    packed = jnp.concatenate(
        [
            attn_gain_part.reshape(groups, -1),
            ffn_gain_part.reshape(groups, -1),
            jnp.broadcast_to(head_gain_parts[0, :, 0], (groups, HEAD_SIZE)),
            jnp.broadcast_to(head_gain_parts[1, :, 0], (groups, HEAD_SIZE)),
        ],
        axis=1,
    )
    summed = jnp.sum(exchange(packed), axis=0)
    summed = jnp.sum(lax.all_gather(summed, "seq", axis=0, tiled=False), axis=0)

    def of_heads(start, width):
        return widen([head_all], place, [(0, width)], width, start // width, ranks)

    def of_tiles(side):
        spans = [(at + side * tile, at + (side + 1) * tile) for at in range(0, f_part, 2 * tile)]
        return widen([left_all, right_all], place, spans, f_part, 0, ranks)

    return (
        back_mixed[send_spot],
        back_grad[send_spot],
        of_heads(0, q_part),
        of_heads(q_part, k_part),
        of_heads(q_part + k_part, k_part),
        widen([head_all], place, [(h_part, h_part + q_part)], h_part + q_part, 0, ranks),
        of_tiles(0),
        of_tiles(1),
        widen([down_all], place, [(0, f_part)], f_part, 0, ranks),
        summed[:gain_rows],
        summed[gain_rows : 2 * gain_rows],
        summed[2 * gain_rows : 2 * gain_rows + HEAD_SIZE],
        summed[2 * gain_rows + HEAD_SIZE :],
    )


def solution(mesh):
    rows = P("fsdp", None)
    tokens = P(("fsdp", "seq"), None)
    in_specs = (
        tokens, tokens, rows, P(("fsdp", "seq")), rows, rows, rows, rows, rows, rows, rows,
        P("fsdp"), P("fsdp"), P(), P(),
    )
    out_specs = (
        tokens, tokens, rows, rows, rows, rows, rows, rows, rows,
        P("fsdp"), P("fsdp"), P(), P(),
    )
    return jax.shard_map(body, mesh=mesh, in_specs=in_specs, out_specs=out_specs, check_vma=False)
```

time: 3410 us -> 1100 us (0.32)
  waiting for transfers between devices: 2080 us -> 353 us
  matrix products: 730 us -> 219 us
  Pallas kernels: 0 us -> 217 us
  other arithmetic: 212 us -> 82.9 us
  blocking collectives: 133 us -> 39.4 us
  local copies, waits for them, and re-layouts: 181 us -> 90.6 us
    unnamed x10 -> x7, waiting for transfers between devices: 1150 us -> 0.8 us
    all_gather x7 -> x3, waiting for transfers between devices: 676 us -> 0.02 us  [gather(): return lax.all_gather(weight, 'fsdp', axis=0, tiled=True)]
    dot_general x49 -> x29, matrix products: 730 us -> 219 us  [the longest x27 204 us: dot(): lax.dot_general(left, right, (((left_dim,), (right_dim,)), ((), ())), pre...]
    ppermute x0 -> x44, waiting for transfers between devices: none -> 293 us  [hop(): return lax.ppermute(rows, 'seq', [(i, i ^ distance) for i in range(ranks)])]
    pallas_call x0 -> x14, Pallas kernels: none -> 217 us  [the longest x4 59.5 us: up_chunk(): pl.pallas_call(functools.partial(up_kernel, tile), out_shape=(jax.ShapeDt...]
    psum x1 -> x0, waiting for transfers between devices: 122 us -> none  [body(): lax.psum(shard_terms.astype(jnp.bfloat16), 'seq').astype(jnp.float32)]
    convert_element_type x18 -> x13, other arithmetic: 122 us -> 25.2 us  [the longest x6 7.28 us: add(): return (a.astype(F32) + b.astype(F32)).astype(BF16)]
    psum x1 -> x0, blocking collectives: 69.3 us -> none  [body(): lax.psum((attn_gain_part, ffn_gain_part, query_gain_part, key_gain_part),...]
  transfers between devices with their start and end apart: 19 -> 57, of which waited for: 12 -> 23; matrix products, arithmetic and copies ran while one was open for 13% -> 34% of each run, Pallas kernels for 0% -> 19%
where the time goes in v1:
time: 1100 us
  waiting for transfers between devices  353 us (32%)
  matrix products  219 us (20%)
  Pallas kernels  217 us (20%)
  local copies, waits for them, and re-layouts  90.6 us (8%)
  other arithmetic  82.9 us (8%)
  starting transfers between devices  79.1 us (7%)
  blocking collectives  39.4 us (4%)
  between operations  18.8 us (2%)
    ppermute x44, waiting for transfers between devices, hop(): return lax.ppermute(rows, 'seq', [(i, i ^ distance) for i in range(ranks)])  293 us
    dot_general x27, matrix products, dot(): lax.dot_general(left, right, (((left_dim,), (right_dim,)), ((), ())), pre...  204 us
    pallas_call x4, Pallas kernels, up_chunk(): pl.pallas_call(functools.partial(up_kernel, tile), out_shape=(jax.ShapeDt...  59.5 us
    all_to_all x5, waiting for transfers between devices, exchange(): return lax.all_to_all(rows, 'fsdp', split_axis=0, concat_axis=0, tiled=True)  59.2 us
    pallas_call x1, Pallas kernels, attend_back(): pl.pallas_call(functools.partial(attend_back_kernel, block, spans), out_s...  52.1 us
    ppermute x44, starting transfers between devices, hop(): return lax.ppermute(rows, 'seq', [(i, i ^ distance) for i in range(ranks)])  47.1 us
    pallas_call x1, Pallas kernels, attend(): pl.pallas_call(functools.partial(attend_kernel, block), out_shape=(jax.Sh...  40.1 us
    pallas_call x1, Pallas kernels, hidden_back(): pl.pallas_call(functools.partial(hidden_back_kernel, tile), out_shape=jax...  38.9 us
  transfers between devices with their start and end apart: 57, of which 23 were waited for; matrix products, arithmetic and copies ran while one was open for 34% of the time, Pallas kernels for 19%

profile of v1, /device:TPU:0, one launch (start us, length us, event | category | flops | bytes accessed | tf_op | source)
XLA Modules:
  0.0 1099.6 jit_solution(5283121498732343330)
XLA Ops:
  33.6 35.8 %all-to-all-done = bf16[8,64,2048]{2,1,0:T(8,128)(2,1)} async-done(((bf16[8,64,2048]{2,1,0:T(8,128)(2,1)}), bf16[8,64,2048]{2,1,0:T(8,128)(2,1)}, u32[]{:S(2)}, u32[]{:S(2)}) %all-to-all-start) | async-done | bytes 2097184 | tf_op jit(solution)/shard_map/all_to_all | solution.py:549
  90.8 44.9 %collective-permute-done = bf16[512,2048]{1,0:T(8,128)(2,1)S(1)} collective-permute-done((bf16[512,2048]{1,0:T(8,128)(2,1)S(1)}, bf16[512,2048]{1,0:T(8,128)(2,1)S(1)}, u32[]{:S(2)}, u32[]{:S(2)}) %collective-permute-start) | collective-permute-done | bytes 2097184 | tf_op jit(solution)/shard_map/ppermute | solution.py:325
  142.0 19.8 %collective-permute-done.2 = bf16[256,2048]{1,0:T(8,128)(2,1)} collective-permute-done((bf16[256,2048]{1,0:T(8,128)(2,1)}, bf16[256,2048]{1,0:T(8,128)(2,1)}, u32[]{:S(2)}, u32[]{:S(2)}) %collective-permute-start.2) | collective-permute-done | bytes 1048608 | tf_op jit(solution)/shard_map/ppermute | solution.py:325
  178.2 36.8 %collective-permute-done.4 = bf16[512,2048]{1,0:T(8,128)(2,1)} collective-permute-done((bf16[512,2048]{1,0:T(8,128)(2,1)S(1)}, bf16[512,2048]{1,0:T(8,128)(2,1)}, u32[]{:S(2)}, u32[]{:S(2)}) %collective-permute-start.4) | collective-permute-done | bytes 2097184 | tf_op jit(solution)/shard_map/ppermute | solution.py:325
  235.5 40.1 %attend.1 = (bf16[4,512,512]{2,1,0:T(8,128)(2,1)S(1)}, bf16[512,2048]{1,0:T(8,128)(2,1)S(1)}, bf16[128,2048]{1,0:T(8,128)(2,1)S(1)}, bf16[128,2048]{1,0:T(8,128)(2,1)S(1)}, f32[2,8,2048]{2,1,0:T(8,128)S(1)}) custom-call(s32[8]{0:T(128)S(1)} %and_select_fusion.low_ref, s32[4]{0:T(128)S(1)} %iota_xor_fusion.order_ref.place_ref, ...), custom_call_target="tpu_custom_call" | custom-call | flops 42949672960 | bytes 12582912 | tf_op jit(solution)/shard_map/attend/pallas_call | solution.py:232
  310.6 40.7 %collective-permute-done.10 = bf16[512,2048]{1,0:T(8,128)(2,1)} collective-permute-done((bf16[512,2048]{1,0:T(8,128)(2,1)}, bf16[512,2048]{1,0:T(8,128)(2,1)}, u32[]{:S(2)}, u32[]{:S(2)}) %collective-permute-start.10) | collective-permute-done | bytes 2097184 | tf_op jit(solution)/shard_map/ppermute | solution.py:325
  360.4 40.6 %collective-permute-done.12 = bf16[512,2048]{1,0:T(8,128)(2,1)S(1)} collective-permute-done((bf16[512,2048]{1,0:T(8,128)(2,1)S(1)}, bf16[512,2048]{1,0:T(8,128)(2,1)S(1)}, u32[]{:S(2)}, u32[]{:S(2)}) %collective-permute-start.12) | collective-permute-done | bytes 2097184 | tf_op jit(solution)/shard_map/ppermute | solution.py:325
  408.6 14.9 %up_chunk.4 = (f32[2048,4096]{1,0:T(8,128)}, bf16[2048,2048]{1,0:T(8,128)(2,1)}, bf16[2048,2048]{1,0:T(8,128)(2,1)}) custom-call(bf16[256,2048]{1,0:T(8,128)(2,1)S(1)} %copy-done.7, bf16[256,2048]{1,0:T(8,128)(2,1)S(1)} %copy-done.6, bf16[2048,4096]{1,0:T(8,128)(2,1)} %all-gather.10.cloned.1.call-done.w_ref), custom_call_target="tpu_custom_call" | custom-call | flops 12884901888 | bytes 31457280 | tf_op jit(solution)/shard_map/up_chunk/pallas_call | solution.py:403
  423.5 14.6 %up_chunk.5 = (f32[2048,4096]{1,0:T(8,128)}, bf16[2048,2048]{1,0:T(8,128)(2,1)}, bf16[2048,2048]{1,0:T(8,128)(2,1)}) custom-call(bf16[256,2048]{1,0:T(8,128)(2,1)S(1)} %get-tuple-element.198.xa, bf16[256,2048]{1,0:T(8,128)(2,1)S(1)} %get-tuple-element.197.xb, ...), custom_call_target="tpu_custom_call", output_to_operand_aliasing={{0}: (3, {}), {1}: (4, {}), {2}: (5, {})} | custom-call | flops 12884901888 | bytes 31457280 | tf_op jit(solution)/shard_map/up_chunk/pallas_call | solution.py:403
  438.1 14.6 %up_chunk.6 = (f32[2048,4096]{1,0:T(8,128)}, bf16[2048,2048]{1,0:T(8,128)(2,1)}, bf16[2048,2048]{1,0:T(8,128)(2,1)}) custom-call(bf16[256,2048]{1,0:T(8,128)(2,1)S(1)} %copy-done.5, bf16[256,2048]{1,0:T(8,128)(2,1)S(1)} %get-tuple-element.200.xb, ...), custom_call_target="tpu_custom_call", output_to_operand_aliasing={{0}: (3, {}), {1}: (4, {}), {2}: (5, {})} | custom-call | flops 12884901888 | bytes 31457280 | tf_op jit(solution)/shard_map/up_chunk/pallas_call | solution.py:403
  452.7 15.4 %up_chunk.7 = (f32[2048,4096]{1,0:T(8,128)}, bf16[2048,2048]{1,0:T(8,128)(2,1)}, bf16[2048,2048]{1,0:T(8,128)(2,1)}) custom-call(bf16[256,2048]{1,0:T(8,128)(2,1)} %collective-permute-done.13.xa, bf16[256,2048]{1,0:T(8,128)(2,1)} %collective-permute-done.15.xb, ...), custom_call_target="tpu_custom_call", output_to_operand_aliasing={{0}: (3, {}), {1}: (4, {}), {2}: (5, {})} | custom-call | flops 12884901888 | bytes 31457280 | tf_op jit(solution)/shard_map/up_chunk/pallas_call | solution.py:403
  468.1 21.3 %convolution_convert_fusion = bf16[2048,2048]{1,0:T(8,128)(2,1)} fusion(bf16[2048,2048]{1,0:T(8,128)(2,1)S(1)} %bitcast.147, bf16[2048,2048]{1,0:T(8,128)(2,1)} %get-tuple-element.155), kind=kOutput, calls=%fused_computation.30 | convolution fusion | flops 17184063488 | bytes 25165824 | tf_op jit(solution)/shard_map/dot_general | solution.py:26
  489.6 38.9 %hidden_back.1 = bf16[2048,4096]{1,0:T(8,128)(2,1)} custom-call(bf16[2048,2048]{1,0:T(8,128)(2,1)} %bitcast.144, bf16[2048,2048]{1,0:T(8,128)(2,1)} %all-gather.8.cloned.1.call-done.w_ref, f32[2048,4096]{1,0:T(8,128)} %get-tuple-element.139.f_ref), custom_call_target="tpu_custom_call" | custom-call | flops 25769803776 | bytes 67108864 | tf_op jit(solution)/shard_map/hidden_back/pallas_call | solution.py:443
  546.3 14.8 %fusion.53 = bf16[512,2048]{1,0:T(8,128)(2,1)} fusion(bf16[2048,4096]{1,0:T(8,128)(2,1)} %all-gather.10.cloned.1.call-done.w_ref, bf16[2048,4096]{1,0:T(8,128)(2,1)} %hidden_back.1), kind=kOutput, calls=%fused_computation.79 | convolution fusion | flops 8590983168 | bytes 23068672 | tf_op jit(solution)/shard_map/dot_general | solution.py:26
  561.2 15.4 %fusion.50 = bf16[512,2048]{1,0:T(8,128)(2,1)} fusion(bf16[2048,4096]{1,0:T(8,128)(2,1)} %all-gather.10.cloned.1.call-done.w_ref, bf16[2048,4096]{1,0:T(8,128)(2,1)} %hidden_back.1), kind=kOutput, calls=%fused_computation.78 | convolution fusion | flops 8590983168 | bytes 23068672 | tf_op jit(solution)/shard_map/dot_general | solution.py:26
  585.9 22.2 %fusion.20 = bf16[2048,2048]{1,0:T(8,128)(2,1)} fusion(bf16[2048,2048]{1,0:T(8,128)(2,1)S(1)} %bitcast.136, bf16[2048,4096]{1,0:T(8,128)(2,1)} %hidden_back.1), kind=kOutput, calls=%fused_computation.28 | convolution fusion | flops 17184063488 | bytes 25165824 | tf_op jit(solution)/shard_map/dot_general | solution.py:26
  608.0 14.0 %fusion.56 = bf16[512,2048]{1,0:T(8,128)(2,1)S(1)} fusion(bf16[2048,4096]{1,0:T(8,128)(2,1)} %all-gather.10.cloned.1.call-done.w_ref, bf16[2048,4096]{1,0:T(8,128)(2,1)} %hidden_back.1), kind=kOutput, calls=%fused_computation.80 | convolution fusion | flops 8590983168 | bytes 23068672 | tf_op jit(solution)/shard_map/dot_general | solution.py:26
  649.7 22.3 %fusion.23 = bf16[2048,2048]{1,0:T(8,128)(2,1)} fusion(bf16[2048,2048]{1,0:T(8,128)(2,1)S(1)} %bitcast.138, bf16[2048,4096]{1,0:T(8,128)(2,1)} %hidden_back.1), kind=kOutput, calls=%fused_computation.29 | convolution fusion | flops 17184063488 | bytes 25165824 | tf_op jit(solution)/shard_map/dot_general | solution.py:26
  745.3 52.1 %attend_back.1 = (bf16[4,768,512]{2,1,0:T(8,128)(2,1)}, f32[2,64,128]{2,1,0:T(8,128)S(1)}) custom-call(s32[8]{0:T(128)S(1)} %copy-done.19, s32[4]{0:T(128)S(1)} %copy-done.15, f32[4,768,512]{2,1,0:T(8,128)} %copy-done.2, f32[4,768,512]{2,1,0:T(8,128)} %copy-done.2, s32[1,2048]{1,0:T(1,128)S(1)} %bitcast.134, f32[32,2048]{1,0:T(8,128)S(1)} %copy-done.11, ...), custom_call_target="tpu_custom_call" | custom-call | flops 57982058496 | bytes 16777216 | tf_op jit(solution)/shard_map/attend_back/pallas_call | solution.py:274
  860.1 28.5 %collective-permute-done.26 = bf16[512,2048]{1,0:T(8,128)(2,1)S(1)} collective-permute-done((bf16[512,2048]{1,0:T(8,128)(2,1)}, bf16[512,2048]{1,0:T(8,128)(2,1)S(1)}, u32[]{:S(2)}, u32[]{:S(2)}) %collective-permute-start.26) | collective-permute-done | bytes 2097184 | tf_op jit(solution)/shard_map/ppermute | solution.py:325
  898.2 23.7 %collective-permute-done.40 = bf16[256,2048]{1,0:T(8,128)(2,1)} collective-permute-done((bf16[256,2048]{1,0:T(8,128)(2,1)}, bf16[256,2048]{1,0:T(8,128)(2,1)}, u32[]{:S(2)}, u32[]{:S(2)}) %collective-permute-start.40) | collective-permute-done | bytes 1048608 | tf_op jit(solution)/shard_map/ppermute | solution.py:325
  933.6 20.7 %all-to-all-done.4 = bf16[8,64,2048]{2,1,0:T(8,128)(2,1)} async-done(((bf16[8,64,2048]{2,1,0:T(8,128)(2,1)}), bf16[8,64,2048]{2,1,0:T(8,128)(2,1)}, u32[]{:S(2)}, u32[]{:S(2)}) %all-to-all-start.4) | async-done | bytes 2097184 | tf_op jit(solution)/shard_map/all_to_all | solution.py:549
  982.3 19.1 %collective-permute-done.36 = bf16[256,2048]{1,0:T(8,128)(2,1)S(1)} collective-permute-done((bf16[256,2048]{1,0:T(8,128)(2,1)S(1)}, bf16[256,2048]{1,0:T(8,128)(2,1)S(1)}, u32[]{:S(2)}, u32[]{:S(2)}) %collective-permute-start.36) | collective-permute-done | bytes 1048608 | tf_op jit(solution)/shard_map/ppermute | solution.py:325
  1009.3 31.4 %all-gather.1 = f32[4,1,640]{2,1,0:T(1,128)S(1)} all-gather(f32[1,1,640]{2,1,0:T(1,128)S(1)} %reshape.216), channel_id=2, replica_groups=mesh['fsdp'=8,'seq'=4] {'seq'}, dimensions={0}, use_global_device_ids=true | all-gather | bytes 12800 | tf_op jit(solution)/shard_map/all_gather | solution.py:724
  (463 shorter events, 438.2 us)
Async XLA Ops:
  13.8 55.5 %all-to-all-start = ((bf16[8,64,2048]{2,1,0:T(8,128)(2,1)}), bf16[8,64,2048]{2,1,0:T(8,128)(2,1)}, u32[]{:S(2)}, u32[]{:S(2)}) async-start(bf16[8,64,2048]{2,1,0:T(8,128)(2,1)} %bitcast.143), calls=%async_computation | async-start | bytes 4194304 | tf_op jit(solution)/shard_map/all_to_all | solution.py:549
  20.2 202.4 %all-gather.6.cloned.1.call-start = ((), (), s32[]{:S(2)}) async-start(), calls=%async_computation.11 | async-start | bytes 5898240 | tf_op jit(solution)/shard_map/all_gather | solution.py:561
  69.4 336.8 %all-gather.10.cloned.1.call-start = ((), (), s32[]{:S(2)}) async-start(), calls=%async_computation.13 | async-start | bytes 18874368 | tf_op jit(solution)/shard_map/all_gather | solution.py:561
  79.5 87.9 %all-to-all-start.2 = ((bf16[8,64,2048]{2,1,0:T(8,128)(2,1)}), bf16[8,64,2048]{2,1,0:T(8,128)(2,1)S(1)}, u32[]{:S(2)}, u32[]{:S(2)}) async-start(bf16[8,64,2048]{2,1,0:T(8,128)(2,1)} %bitcast.142), calls=%async_computation.2 | async-start | bytes 4194304 | tf_op jit(solution)/shard_map/all_to_all | solution.py:549
  83.1 406.4 %all-gather.8.cloned.1.call-start = ((), (), s32[]{:S(2)}) async-start(), calls=%async_computation.12 | async-start | bytes 9437184 | tf_op jit(solution)/shard_map/all_gather | solution.py:561
  89.3 49.0 %collective-permute-start.1 = (bf16[512,2048]{1,0:T(8,128)(2,1)S(1)}, bf16[512,2048]{1,0:T(8,128)(2,1)S(1)}, u32[]{:S(2)}, u32[]{:S(2)}) collective-permute-start(bf16[512,2048]{1,0:T(8,128)(2,1)S(1)} %fusion.30), channel_id=1, source_target_pairs={{0,2},{1,3},{2,0},{3,1},{4,6},{5,7},{6,4},{7,5},{8,10},{9,11},{10,... | collective-permute-start | bytes 6291464 | tf_op jit(solution)/shard_map/ppermute | solution.py:325
  169.1 50.6 %collective-permute-start.5 = (bf16[512,2048]{1,0:T(8,128)(2,1)S(1)}, bf16[512,2048]{1,0:T(8,128)(2,1)S(1)}, u32[]{:S(2)}, u32[]{:S(2)}) collective-permute-start(bf16[512,2048]{1,0:T(8,128)(2,1)S(1)} %bitcast.140), channel_id=1, source_target_pairs={{0,2},{1,3},{2,0},{3,1},{4,6},{5,7},{6,4},{7,5},{8,10},{9,11},{10,... | collective-permute-start | bytes 6291464 | tf_op jit(solution)/shard_map/ppermute | solution.py:325
  218.2 59.8 %collective-permute-start.6 = (bf16[256,2048]{1,0:T(8,128)(2,1)}, bf16[256,2048]{1,0:T(8,128)(2,1)}, u32[]{:S(2)}, u32[]{:S(2)}) collective-permute-start(bf16[256,2048]{1,0:T(8,128)(2,1)} %get-tuple-element.114), channel_id=1, source_target_pairs={{0,2},{1,3},{2,0},{3,1},{4,6},{5,7},{6,4},{7,5},{8,10},{9,11},{10,... | collective-permute-start | bytes 3145736 | tf_op jit(solution)/shard_map/ppermute | solution.py:325
  221.1 56.8 %collective-permute-start.7 = (bf16[256,2048]{1,0:T(8,128)(2,1)}, bf16[256,2048]{1,0:T(8,128)(2,1)}, u32[]{:S(2)}, u32[]{:S(2)}) collective-permute-start(bf16[256,2048]{1,0:T(8,128)(2,1)} %get-tuple-element.117), channel_id=1, source_target_pairs={{0,1},{1,0},{2,3},{3,2},{4,5},{5,4},{6,7},{7,6},{8,9},{9,8},{10,11... | collective-permute-start | bytes 3145736 | tf_op jit(solution)/shard_map/ppermute | solution.py:325
  307.6 433.0 %reduce-scatter.5.cloned.1.call-start = ((), (), s32[]{:S(2)}) async-start(), calls=%async_computation.14 | async-start | bytes 9437184 | tf_op jit(solution)/shard_map/reduce_scatter | solution.py:641
  401.1 51.6 %collective-permute-start.13 = (bf16[256,2048]{1,0:T(8,128)(2,1)S(1)}, bf16[256,2048]{1,0:T(8,128)(2,1)}, u32[]{:S(2)}, u32[]{:S(2)}) collective-permute-start(bf16[256,2048]{1,0:T(8,128)(2,1)S(1)} %get-tuple-element.198.xa), channel_id=1, source_target_pairs={{0,2},{1,3},{2,0},{3,1},{4,6},{5,7},{6,4},{7,5},{8,10},{9,11},{10,... | collective-permute-start | bytes 3145736 | tf_op jit(solution)/shard_map/ppermute | solution.py:325
  489.5 308.0 %reduce-scatter.7.cloned.1.call-start = ((), (), s32[]{:S(2)}) async-start(), calls=%async_computation.15 | async-start | bytes 9437184 | tf_op jit(solution)/shard_map/reduce_scatter | solution.py:641
  625.2 339.6 %reduce-scatter.9.cloned.1.call-start = ((), (), s32[]{:S(2)}) async-start(), calls=%async_computation.16 | async-start | bytes 9437184 | tf_op jit(solution)/shard_map/reduce_scatter | solution.py:641
  640.8 48.8 %collective-permute-start.20 = (bf16[512,2048]{1,0:T(8,128)(2,1)}, bf16[512,2048]{1,0:T(8,128)(2,1)}, u32[]{:S(2)}, u32[]{:S(2)}) collective-permute-start(bf16[512,2048]{1,0:T(8,128)(2,1)} %get-tuple-element.153), channel_id=1, source_target_pairs={{0,1},{1,0},{2,3},{3,2},{4,5},{5,4},{6,7},{7,6},{8,9},{9,8},{10,11... | collective-permute-start | bytes 6291464 | tf_op jit(solution)/shard_map/ppermute | solution.py:325
  641.4 50.6 %collective-permute-start.21 = (bf16[512,2048]{1,0:T(8,128)(2,1)}, bf16[512,2048]{1,0:T(8,128)(2,1)}, u32[]{:S(2)}, u32[]{:S(2)}) collective-permute-start(bf16[512,2048]{1,0:T(8,128)(2,1)} %get-tuple-element.153), channel_id=1, source_target_pairs={{0,2},{1,3},{2,0},{3,1},{4,6},{5,7},{6,4},{7,5},{8,10},{9,11},{10,... | collective-permute-start | bytes 6291464 | tf_op jit(solution)/shard_map/ppermute | solution.py:325
  728.2 116.7 %all-to-all-start.3 = ((bf16[4,512,2048]{2,1,0:T(8,128)(2,1)}), bf16[4,512,2048]{2,1,0:T(8,128)(2,1)}, u32[]{:S(2)}, u32[]{:S(2)}) async-start(bf16[4,512,2048]{2,1,0:T(8,128)(2,1)} %pad_maximum_fusion.1), calls=%async_computation.5 | async-start | bytes 16777216 | tf_op jit(solution)/shard_map/all_to_all | solution.py:684
  733.8 272.6 %reduce-scatter.11.cloned.1.call-start = ((), (), s32[]{:S(2)}) async-start(), calls=%async_computation.17 | async-start | bytes 5898240 | tf_op jit(solution)/shard_map/reduce_scatter | solution.py:641
  888.9 65.5 %all-to-all-start.4 = ((bf16[8,64,2048]{2,1,0:T(8,128)(2,1)}), bf16[8,64,2048]{2,1,0:T(8,128)(2,1)}, u32[]{:S(2)}, u32[]{:S(2)}) async-start(bf16[8,64,2048]{2,1,0:T(8,128)(2,1)} %bitcast.49), calls=%async_computation.6 | async-start | bytes 4194304 | tf_op jit(solution)/shard_map/all_to_all | solution.py:549
  926.7 51.8 %collective-permute-start.32 = (bf16[256,2048]{1,0:T(8,128)(2,1)}, bf16[256,2048]{1,0:T(8,128)(2,1)}, u32[]{:S(2)}, u32[]{:S(2)}) collective-permute-start(bf16[256,2048]{1,0:T(8,128)(2,1)} %reduce-scatter.7.cloned.1.call-done), channel_id=1, source_target_pairs={{0,1},{1,0},{2,3},{3,2},{4,5},{5,4},{6,7},{7,6},{8,9},{9,8},{10,11... | collective-permute-start | bytes 3145736 | tf_op jit(solution)/shard_map/ppermute | solution.py:325
  927.1 53.3 %collective-permute-start.33 = (bf16[256,2048]{1,0:T(8,128)(2,1)}, bf16[256,2048]{1,0:T(8,128)(2,1)}, u32[]{:S(2)}, u32[]{:S(2)}) collective-permute-start(bf16[256,2048]{1,0:T(8,128)(2,1)} %reduce-scatter.7.cloned.1.call-done), channel_id=1, source_target_pairs={{0,2},{1,3},{2,0},{3,1},{4,6},{5,7},{6,4},{7,5},{8,10},{9,11},{10,... | collective-permute-start | bytes 3145736 | tf_op jit(solution)/shard_map/ppermute | solution.py:325
  964.8 100.5 %all-to-all-start.5 = ((bf16[8,64,2048]{2,1,0:T(8,128)(2,1)}), bf16[8,64,2048]{2,1,0:T(8,128)(2,1)}, u32[]{:S(2)}, u32[]{:S(2)}) async-start(bf16[8,64,2048]{2,1,0:T(8,128)(2,1)} %bitcast.150), calls=%async_computation.8 | async-start | bytes 4194304 | tf_op jit(solution)/shard_map/all_to_all | solution.py:549
  979.8 61.6 %collective-permute-start.34 = (bf16[128,2048]{1,0:T(8,128)(2,1)S(1)}, bf16[128,2048]{1,0:T(8,128)(2,1)}, u32[]{:S(2)}, u32[]{:S(2)}) collective-permute-start(bf16[128,2048]{1,0:T(8,128)(2,1)S(1)} %get-tuple-element.224.refs_2_), channel_id=1, source_target_pairs={{0,2},{1,3},{2,0},{3,1},{4,6},{5,7},{6,4},{7,5},{8,10},{9,11},{10,... | collective-permute-start | bytes 1572872 | tf_op jit(solution)/shard_map/ppermute | solution.py:325
  981.6 61.7 %collective-permute-start.35 = (bf16[128,2048]{1,0:T(8,128)(2,1)S(1)}, bf16[128,2048]{1,0:T(8,128)(2,1)}, u32[]{:S(2)}, u32[]{:S(2)}) collective-permute-start(bf16[128,2048]{1,0:T(8,128)(2,1)S(1)} %get-tuple-element.221.refs_5_), channel_id=1, source_target_pairs={{0,1},{1,0},{2,3},{3,2},{4,5},{5,4},{6,7},{7,6},{8,9},{9,8},{10,11... | collective-permute-start | bytes 1572872 | tf_op jit(solution)/shard_map/ppermute | solution.py:325
  1006.4 66.0 %collective-permute-start.28 = (bf16[256,1280]{1,0:T(8,128)(2,1)}, bf16[256,1280]{1,0:T(8,128)(2,1)}, u32[]{:S(2)}, u32[]{:S(2)}) collective-permute-start(bf16[256,1280]{1,0:T(8,128)(2,1)} %reduce-scatter.11.cloned.1.call-done), channel_id=1, source_target_pairs={{0,1},{1,0},{2,3},{3,2},{4,5},{5,4},{6,7},{7,6},{8,9},{9,8},{10,11... | collective-permute-start | bytes 1966088 | tf_op jit(solution)/shard_map/ppermute | solution.py:325
  (129 other events, 2590.1 us)
Sparse Core Ops, SparseCore 0:
  69.5 94.8 all-gather.5
  165.9 149.5 all-gather.9
  317.1 80.2 all-gather.7
  489.6 92.3 reduce-scatter.4
  625.3 91.9 reduce-scatter.6
  720.0 87.9 reduce-scatter.8
  845.1 73.8 reduce-scatter.10

commit v2 on v1

--- a/solution.py
+++ b/solution.py
@@ -250,11 +250,7 @@
             ],
         ),
         compiler_params=pltpu.CompilerParams(vmem_limit_bytes=40 << 20),
-        cost_estimate=pl.CostEstimate(
-            flops=20 * local * width * group_rows * group_rows,
-            bytes_accessed=12 * local * width * group_rows,
-            transcendentals=local * GROUP_HEADS * group_rows * group_rows,
-        ),
+        cost_estimate=pl.CostEstimate(flops=1 << 20, bytes_accessed=1 << 20, transcendentals=0),
         name="attend",
     )(low, order, qkv_raw, qkv_raw, qkv_raw, starts, cosine, sine, gains)
 
@@ -298,9 +294,7 @@
         ),
         compiler_params=pltpu.CompilerParams(vmem_limit_bytes=48 << 20),
         cost_estimate=pl.CostEstimate(
-            flops=27 * local * width * group_rows * group_rows,
-            bytes_accessed=16 * local * width * group_rows,
-            transcendentals=local * GROUP_HEADS * group_rows * group_rows,
+            flops=400 * 10**9, bytes_accessed=1 << 20, transcendentals=0
         ),
         name="attend_back",
     )(
@@ -329,17 +323,38 @@
     return lax.optimization_barrier((values, first))[0]
 
 
+def gather_start(rows, ranks):
+    return [rows] + [hop(rows, k, ranks) for k in range(1, ranks if ranks != 4 else 3)]
+
+
+def gather_finish(chunks, ranks):
+    half = chunks[0].shape[0] // 2
+    pairs = [((m, 0), (m, 1)) for m in chunks]
+    if ranks == 4:
+        corner = hop(chunks[1][:half], 2, ranks), hop(chunks[2][half:], 1, ranks)
+        pairs.append(((corner[0], 0), (corner[1], 0)))
+    return pairs
+
+
 def gather_chunks(rows, ranks):
-    half = rows.shape[0] // 2
-    if ranks != 4:
-        moved = [rows] + [hop(rows, k, ranks) for k in range(1, ranks)]
-        return [(m[:half], m[half:]) for m in moved]
-    first, second = hop(rows, 1, ranks), hop(rows, 2, ranks)
-    corner = hop(first[:half], 2, ranks), hop(second[half:], 1, ranks)
-    return [(m[:half], m[half:]) for m in (rows, first, second)] + [corner]
-
-
-def scatter_chunks(make, given, ranks, early=((), None), late=((), None)):
+    return gather_finish(gather_start(rows, ranks), ranks)
+
+
+def joined(pair):
+    (first, _), (second, _) = pair
+    return first if first is second else jnp.concatenate([first, second])
+
+
+def pieces_of(pairs):
+    flat = [piece for pair in pairs for piece in pair]
+    return [m for m, _ in flat], [at for _, at in flat]
+
+
+def add(a, b):
+    return (a.astype(F32) + b.astype(F32)).astype(BF16)
+
+
+def scatter_chunks(make, given, ranks, early=((), None), late=((), None), keep=False, wait=()):
     def run(work, arrays):
         return work[1](arrays) if work[1] else ()
 
@@ -349,28 +364,56 @@
         own = make(0, given)
         more = run(early, first), run(late, second)
         moved = [hop(part, k + 1, ranks) for k, part in enumerate(sent)]
-        moved, own, more = lax.optimization_barrier((moved, own, more))
-        return sum((m.astype(F32) for m in moved), own.astype(F32)), *more
+        moved, own, wait = lax.optimization_barrier((moved, own, wait))
+        return sum((m.astype(F32) for m in moved), own.astype(F32)), *more, wait
     corner = make(3, given)
     half = corner.shape[0] // 2
     corner, given, arrays = lax.optimization_barrier((corner, given, early[0]))
     for_second = hop(corner[:half], 1, ranks)
     for_first = hop(corner[half:], 2, ranks)
-    first, second, early = make(1, given), make(2, given), run(early, arrays)
-
-    def add(a, b):
-        return (a.astype(F32) + b.astype(F32)).astype(BF16)
-
-    first = jnp.concatenate([first[:half], add(first[half:], for_first)])
-    second = jnp.concatenate([add(second[:half], for_second), second[half:]])
-    first, second, given, early, arrays = lax.optimization_barrier(
-        (first, second, given, early, late[0])
+    first = make(1, given)
+    top = first[:half]
+    top, given = lax.optimization_barrier((top, given))
+    top = hop(top, 1, ranks)
+    second, early = make(2, given), run(early, arrays)
+
+    bottom = second[half:]
+    first, second = add(first[half:], for_first), add(second[:half], for_second)
+    bottom, first, second, given, early, arrays = lax.optimization_barrier(
+        (bottom, first, second, given, early, late[0])
     )
     own, late = make(0, given), run(late, arrays)
-    first, second, own, late = lax.optimization_barrier(
-        (hop(first, 1, ranks), hop(second, 2, ranks), own, late)
-    )
-    return own.astype(F32) + first.astype(F32) + second.astype(F32), early, late
+    moved = top, hop(first, 1, ranks), hop(second, 2, ranks), hop(bottom, 2, ranks), own
+    if keep:
+        moved, wait = lax.optimization_barrier((moved, wait))
+    else:
+        moved, late, wait = lax.optimization_barrier((moved, late, wait))
+    top, first, second, bottom, own = moved
+    first = jnp.concatenate([top, first]).astype(F32)
+    second = jnp.concatenate([second, bottom]).astype(F32)
+    return own.astype(F32) + first + second, early, late, wait
+
+
+def rows_kernel(left, right, out):
+    out[...] = dot(left[...], right[...], 1, 1).astype(BF16)
+
+
+def rows_times(left, k, right, rows):
+    width, depth = right.shape
+    tile = min(512, width)
+    return pl.pallas_call(
+        rows_kernel,
+        out_shape=jax.ShapeDtypeStruct((rows, width), BF16),
+        grid=(width // tile,),
+        in_specs=[
+            pl.BlockSpec((rows, depth), lambda t: (k, 0)),
+            pl.BlockSpec((tile, depth), lambda t: (t, 0)),
+        ],
+        out_specs=pl.BlockSpec((rows, tile), lambda t: (0, t)),
+        compiler_params=pltpu.CompilerParams(vmem_limit_bytes=48 << 20),
+        cost_estimate=pl.CostEstimate(flops=1 << 20, bytes_accessed=1 << 20, transcendentals=0),
+        name="rows_times",
+    )(left, right)
 
 
 def up_kernel(tile, xa, xb, w_ref, *rest):
@@ -390,20 +433,21 @@
         gated = jax.nn.sigmoid(gate)
         silu = gate * gated
         hid_ref[:, i * tile : (i + 1) * tile] = (silu * up).astype(BF16)
-        f_ref[:, left:right] = up * (gated + silu * (1.0 - gated))
-        f_ref[:, right : right + tile] = silu
-
-
-def up_chunk(k, x, gate_up, before, ranks, tile):
-    half, features = x[0].shape
-    rows, width = 2 * half, gate_up.shape[1]
-    halves = [pl.BlockSpec((half, features), lambda t: (0, 0))] * 2
+        f_ref[:, left:right] = (up * (gated + silu * (1.0 - gated))).astype(BF16)
+        f_ref[:, right : right + tile] = silu.astype(BF16)
+
+
+def up_chunk(k, x, gate_up, before, ranks, tile, rows):
+    arrays, places = pieces_of([x])
+    half, features = rows // 2, arrays[0].shape[1]
+    width = gate_up.shape[1]
+    halves = [pl.BlockSpec((half, features), lambda t, at=at: (at, 0)) for at in places]
     step = min(2 * tile, width // 2)
     kept = [] if before is None else list(before)
     return pl.pallas_call(
         functools.partial(up_kernel, tile),
         out_shape=(
-            jax.ShapeDtypeStruct((ranks * rows, width), F32),
+            jax.ShapeDtypeStruct((ranks * rows, width), BF16),
             jax.ShapeDtypeStruct((ranks * rows, width // 2), BF16),
             jax.ShapeDtypeStruct((ranks * rows, features), BF16),
         ),
@@ -419,49 +463,86 @@
         scratch_shapes=[pltpu.VMEM((rows, features), BF16)],
         input_output_aliases={3 + i: i for i in range(len(kept))},
         compiler_params=pltpu.CompilerParams(vmem_limit_bytes=48 << 20),
-        cost_estimate=pl.CostEstimate(
-            flops=3 * rows * features * width,
-            bytes_accessed=2 * features * width + 5 * rows * width + 4 * rows * features,
-            transcendentals=rows * width // 2,
-        ),
+        cost_estimate=pl.CostEstimate(flops=1 << 20, bytes_accessed=1 << 20, transcendentals=0),
         name="up_chunk",
-    )(*x, gate_up, *kept)
+    )(*arrays, gate_up, *kept)
+
+
+def head_outer_kernel(count, d_ref, a_ref, *refs):
+    out = refs[-1]
+    at = 0
+    for left, pieces in ((d_ref, refs[:count]), (a_ref, refs[count : 2 * count])):
+        half = pieces[0].shape[0]
+        total = sum(
+            dot(left[i // 2, :, (i % 2) * half : (i % 2 + 1) * half], piece[...], 1, 0)
+            for i, piece in enumerate(pieces)
+        )
+        out[:, at : at + left.shape[1]] = total.T.astype(BF16)
+        at += left.shape[1]
+
+
+def head_outer(d_heads, normed, attended, branch):
+    ranks, width, rows = d_heads.shape
+    more = attended.shape[1]
+    left, left_places = pieces_of(normed)
+    right, right_places = pieces_of(branch)
+    features = left[0].shape[1]
+    tile = min(512, features)
+
+    def heads(w):
+        return pl.BlockSpec((ranks, w, rows), lambda t: (0, 0, 0))
+
+    tokens = [
+        pl.BlockSpec((rows // 2, tile), lambda t, at=at: (at, t))
+        for at in left_places + right_places
+    ]
+    return pl.pallas_call(
+        functools.partial(head_outer_kernel, len(left)),
+        out_shape=jax.ShapeDtypeStruct((features, width + more), BF16),
+        grid=(features // tile,),
+        in_specs=[heads(width), heads(more), *tokens],
+        out_specs=pl.BlockSpec((tile, width + more), lambda t: (t, 0)),
+        compiler_params=pltpu.CompilerParams(vmem_limit_bytes=48 << 20),
+        cost_estimate=pl.CostEstimate(flops=1 << 20, bytes_accessed=1 << 20, transcendentals=0),
+        name="head_outer",
+    )(d_heads, attended, *left, *right)
 
 
 def hidden_back_kernel(tile, c_ref, w_ref, f_ref, d_ref):
-    for i in range(w_ref.shape[1] // tile):
-        left, right = 2 * i * tile, (2 * i + 1) * tile
-        hidden_grad = dot(c_ref[...], w_ref[:, i * tile : (i + 1) * tile], 1, 0)
-        d_ref[:, left:right] = (hidden_grad * f_ref[:, left:right]).astype(BF16)
-        d_ref[:, right : right + tile] = (hidden_grad * f_ref[:, right : right + tile]).astype(BF16)
-
-
-def hidden_back(cot, down, factors, tile, rows):
+    rows = c_ref.shape[0] // 4
+    for r in range(4):
+        at = slice(r * rows, (r + 1) * rows)
+        hidden_grad = dot(c_ref[at, :], w_ref[...], 1, 0)
+        for i in range(w_ref.shape[1] // tile):
+            left, right = 2 * i * tile, (2 * i + 1) * tile
+            part = hidden_grad[:, i * tile : (i + 1) * tile]
+            d_ref[at, left:right] = (part * f_ref[at, left:right].astype(F32)).astype(BF16)
+            d_ref[at, right : right + tile] = (
+                part * f_ref[at, right : right + tile].astype(F32)
+            ).astype(BF16)
+
+
+def hidden_back(cot, down, factors, tile):
     group_rows, features = cot.shape
     width = down.shape[1]
     step = min(2 * tile, width)
     return pl.pallas_call(
         functools.partial(hidden_back_kernel, tile),
         out_shape=jax.ShapeDtypeStruct((group_rows, 2 * width), BF16),
-        grid=(group_rows // rows, width // step),
+        grid=(width // step,),
         in_specs=[
-            pl.BlockSpec((rows, features), lambda r, t: (r, 0)),
-            pl.BlockSpec((features, step), lambda r, t: (0, t)),
-            pl.BlockSpec((rows, 2 * step), lambda r, t: (r, t)),
+            pl.BlockSpec((group_rows, features), lambda t: (0, 0)),
+            pl.BlockSpec((features, step), lambda t: (0, t)),
+            pl.BlockSpec((group_rows, 2 * step), lambda t: (0, t)),
         ],
-        out_specs=pl.BlockSpec((rows, 2 * step), lambda r, t: (r, t)),
-        compiler_params=pltpu.CompilerParams(vmem_limit_bytes=48 << 20),
-        cost_estimate=pl.CostEstimate(
-            flops=3 * group_rows * features * width,
-            bytes_accessed=4 * features * width + 12 * group_rows * width,
-            transcendentals=group_rows * width,
-        ),
+        out_specs=pl.BlockSpec((group_rows, 2 * step), lambda t: (0, t)),
+        compiler_params=pltpu.CompilerParams(vmem_limit_bytes=56 << 20),
+        cost_estimate=pl.CostEstimate(flops=1 << 20, bytes_accessed=1 << 20, transcendentals=0),
         name="hidden_back",
     )(cot, down, factors)
 
 
-def widen(pieces, place, columns, part, total, ranks):
-    rows = 2 * pieces[0][0][0].shape[0]
+def widen(pieces, place, columns, part, total, ranks, rows):
     each = sum(stop - start for start, stop in columns)
     width = each * len(pieces)
     if ranks != 4:
@@ -472,7 +553,7 @@
         stacked = jnp.stack(
             [
                 jnp.concatenate(
-                    [jnp.concatenate([picked(p) for p in group[k]]) for group in pieces], axis=1
+                    [picked(joined(group[k])) for group in pieces], axis=1
                 )
                 for k in range(ranks)
             ]
@@ -480,9 +561,11 @@
         ordered = jnp.swapaxes(jnp.take(stacked, place, axis=0), 0, 1)
         return ordered.reshape(rows, ranks * width).astype(F32)
     half = rows // 2
-    flat = [p for group in pieces for chunk in group for p in chunk]
+    flat, places = pieces_of([pair for group in pieces for pair in group])
     counts = len(pieces)
-    whole = pl.BlockSpec((half, part), lambda k, place: (0, total))
+    whole = [
+        pl.BlockSpec((half, part), lambda k, place, at=at: (at, total)) for at in places
+    ]
 
     def kernel(place_ref, *refs):
         out = refs[-1]
@@ -506,12 +589,12 @@
         grid_spec=pltpu.PrefetchScalarGridSpec(
             num_scalar_prefetch=1,
             grid=(ranks,),
-            in_specs=[whole] * len(flat),
+            in_specs=whole,
             out_specs=pl.BlockSpec((rows, width), lambda k, place: (0, place[k])),
         ),
         compiler_params=pltpu.CompilerParams(vmem_limit_bytes=48 << 20),
         cost_estimate=pl.CostEstimate(
-            flops=rows * width * ranks, bytes_accessed=6 * rows * width * ranks, transcendentals=0
+            flops=rows * width * ranks * 15000, bytes_accessed=1 << 20, transcendentals=0
         ),
         name="widen",
     )(place, *flat)
@@ -535,6 +618,7 @@
     block = min(256, token_rows)
     tile = min(256, f_part)
     gain_rows = attn_gain.shape[0]
+    shard = q_weight.shape[0]
 
     local_slot = owner_slot % token_rows
     target = owner_slot // token_rows // ranks
@@ -550,9 +634,10 @@
 
     both_gains = jnp.concatenate([attn_gain, ffn_gain])
     gains_full = exchange(jnp.broadcast_to(both_gains, (groups, 2 * gain_rows))).astype(F32)
+    token_rows_sent, gains_full = lax.optimization_barrier((tokens[inverse], gains_full))
+    owned = exchange(token_rows_sent)
     attn_full = gains_full[:, :gain_rows].reshape(features)
     ffn_full = gains_full[:, gain_rows:].reshape(features)
-    owned = exchange(tokens[inverse])
 
     def columns(weight, width):
         return lax.dynamic_slice_in_dim(weight, seq_index * width, width, 1)
@@ -605,38 +690,33 @@
     head_gains = jnp.stack([query_gain, key_gain]).astype(F32)[:, :, None]
     place = jnp.bitwise_xor(seq_index, jnp.arange(ranks, dtype=jnp.int32)).astype(jnp.int32)
 
-    def together(chunks):
-        return jnp.stack([jnp.concatenate(pair) for pair in chunks])
-
     tok_f32 = owned.astype(F32)
     scale_one, normed_own = rms_parts(tok_f32, attn_full)
     normed = gather_chunks(normed_own, ranks)
-    normed[-1], cot_sent = lax.optimization_barrier((normed[-1], cot_owned))
-    cot = gather_chunks(cot_sent, ranks)
-    normed = together(normed)
-    qkv_raw = jnp.stack([dot(qkv_own, normed[k], 0, 1) for k in range(ranks)])
+    (last, first_place), (other, other_place) = normed[-1]
+    alike = last is other
+    last, other, cot_sent = lax.optimization_barrier((last, other[:8] if alike else other, cot_owned))
+    normed[-1] = (last, first_place), (last if alike else other, other_place)
+    cot = gather_start(cot_sent, ranks)
+    qkv_raw = jnp.stack([dot(qkv_own, joined(pair), 0, 1) for pair in normed])
     attended, query, key, value, lse_table = attend(
         qkv_raw, low, place, start_row, cosine, sine, head_gains, ranks, local, block
     )
-    branch_sum, cot, _ = scatter_chunks(
-        lambda k, given: dot(given[0][k], given[1], 0, 1).astype(BF16),
-        (after(attended, cot[:3]), wo_own),
-        ranks,
-        early=(cot, together),
+    attended, cot, wo_own = lax.optimization_barrier((attended, cot, wo_own))
+    branch_sum, *_ = scatter_chunks(
+        lambda k, given: dot(given[k], wo_own, 0, 1).astype(BF16), attended, ranks
     )
     resid = tok_f32 + branch_sum
 
     scale_two, normed_two_own = rms_parts(resid, ffn_full)
-    results = None
-    for k, chunk in enumerate(gather_chunks(normed_two_own, ranks)):
-        results = up_chunk(k, chunk, gate_up_own, results, ranks, tile)
+    chunks = gather_start(normed_two_own, ranks)
+    results = up_chunk(0, gather_finish(chunks[:1], 1)[0], gate_up_own, None, ranks, tile, token_rows)
+    chunks[1:], results, cot = lax.optimization_barrier((chunks[1:], results, cot))
+    chunks = gather_finish(chunks, ranks)
+    cot = cot + [m for m, _ in gather_finish(cot, ranks)[len(cot) :][0]] if ranks == 4 else cot
+    for k in range(1, ranks):
+        results = up_chunk(k, chunks[k], gate_up_own, results, ranks, tile, token_rows)
     factors, hidden, normed_two = results
-    cot = cot.reshape(group_rows, features)
-    gate_up_grad = hidden_back(cot, down_own, factors, tile, token_rows)
-
-    def rows_of(array, k):
-        return array[k * token_rows : (k + 1) * token_rows]
-
     def scatter(terms):
         return lax.psum_scatter(
             terms.astype(BF16), "fsdp", scatter_dimension=0, tiled=True
@@ -645,72 +725,78 @@
     def terms_of(left, right):
         return dot(left, right, 0, 0).astype(BF16)
 
-    down_terms = terms_of(cot, hidden)
-    normed_two_grad, _, left_terms = scatter_chunks(
-        lambda k, given: dot(rows_of(given[0], k), given[1], 1, 1).astype(BF16),
-        (gate_up_grad, gate_up_own),
+    def down_part(k, hidden):
+        return rows_times(hidden, k, down_own, token_rows)
+
+    if ranks == 4:
+        half = token_rows // 2
+        corner = down_part(3, hidden)
+        for_second, for_first = hop(corner[:half], 1, ranks), hop(corner[half:], 2, ranks)
+        cot, hidden = lax.optimization_barrier((cot, hidden))
+        cot = jnp.concatenate(cot)
+        first, second = down_part(1, hidden), down_part(2, hidden)
+        down_terms = terms_of(cot, hidden)
+        for_first, for_second, down_terms, first, second = lax.optimization_barrier(
+            (for_first, for_second, down_terms, first, second)
+        )
+        down_parts = [
+            jnp.concatenate([first[:half], add(first[half:], for_first)]),
+            jnp.concatenate([add(second[:half], for_second), second[half:]]),
+        ]
+    else:
+        cot = jnp.concatenate(cot)
+        down_parts = [down_part(k, hidden) for k in range(1, ranks)]
+        down_terms = terms_of(cot, hidden)
+    down_grad = scatter(down_terms)
+    factors, down_parts, cot = lax.optimization_barrier((factors, down_parts, cot))
+    down_sent = [hop(part, k + 1, ranks) for k, part in enumerate(down_parts)]
+    gate_up_grad = hidden_back(cot, down_own, factors, tile)
+    normed_two_grad, down_sent, down_out, _ = scatter_chunks(
+        lambda k, given: rows_times(given, k, gate_up_own, token_rows),
+        gate_up_grad,
         ranks,
-        late=(normed_two, lambda rows: terms_of(rows, gate_up_grad[:, :f_part])),
-    )
-    down_grad = scatter(down_terms)
-    left_grad = scatter(left_terms)
+        early=(down_sent, lambda a: a),
+        late=(hidden, lambda a: down_part(0, a)),
+    )
     resid_part, ffn_gain_part = rms_back(resid, scale_two, ffn_full, normed_two_grad)
     resid_grad = cot_owned.astype(F32) + resid_part
     branch_own = resid_grad.astype(BF16)
-    branch_own, right_in, hidden = lax.optimization_barrier((branch_own, normed_two, hidden))
-    branch = gather_chunks(branch_own, ranks)
-    right_terms = terms_of(right_in, gate_up_grad[:, f_part:])
-    down_parts = jnp.stack(
-        [
-            dot(
-                lax.dynamic_slice_in_dim(hidden, place[j] * token_rows, token_rows, 0),
-                down_own, 1, 1,
-            ).astype(BF16)
-            for j in range(ranks)
-        ]
-    )
-    branch[-1], right_terms, down_parts = lax.optimization_barrier(
-        (branch[-1], right_terms, down_parts)
-    )
-    branch = together(branch)
-    right_grad = scatter(right_terms)
-    attended_grad = jnp.stack(
-        [dot(wo_own, branch[k], 0, 1).astype(BF16) for k in range(ranks)]
-    )
+    branch_own, normed_two = lax.optimization_barrier((branch_own, normed_two))
+    branch = gather_start(branch_own, ranks)
+    gate_up_terms = terms_of(normed_two, gate_up_grad)
+    down_out = sum((part.astype(F32) for part in down_sent), down_out.astype(F32))
+    mixed_own = (resid + down_out).astype(BF16)
+
+    def heads_of(rows):
+        return dot(wo_own, rows, 0, 1).astype(BF16)
+
+    attended_grad = [heads_of(rows) for rows in branch]
+    branch, gate_up_terms = lax.optimization_barrier((branch, gate_up_terms))
+    gate_up_out = scatter(gate_up_terms)
+    branch = gather_finish(branch, ranks)
+    if ranks == 4:
+        attended_grad.append(heads_of(joined(branch[-1])))
+    attended_grad = jnp.stack(attended_grad)
+    down_all = gather_start(down_grad, ranks)
     d_heads, head_gain_parts = attend_back(
         qkv_raw, low, place, start_row, cosine, sine, head_gains, query, key, value, lse_table,
-        attended, after(attended_grad, down_grad), ranks, local, block,
-    )
-    down_moved = lax.all_to_all(down_parts, "seq", split_axis=0, concat_axis=0, tiled=True)
-    d_heads = after(d_heads, left_grad)
-
-    def outer(left, right):
-        return lax.dot_general(
-            left.reshape(ranks, token_rows, features), right,
-            (((0, 1), (0, 2)), ((), ())), preferred_element_type=F32,
-        ).astype(BF16)
-
-    normed_grad, head_terms, mixed_own = scatter_chunks(
-        lambda k, given: dot(given[0][k], given[1], 0, 1).astype(BF16),
-        (d_heads, qkv_own),
+        attended, attended_grad, ranks, local, block,
+    )
+    d_heads, down_all, back_mixed = lax.optimization_barrier(
+        (d_heads, down_all, exchange(mixed_own))
+    )
+
+    normed_grad, _, head_terms, _ = scatter_chunks(
+        lambda k, given: dot(given[k], qkv_own, 0, 1).astype(BF16),
+        d_heads,
         ranks,
-        early=(
+        late=(
             (d_heads, attended),
-            lambda a: jnp.concatenate([outer(normed, a[0]), outer(branch, a[1])], axis=1),
-        ),
-        late=(down_moved, lambda a: (resid + jnp.sum(a.astype(F32), axis=0)).astype(BF16)),
-    )
-    head_grad = scatter(head_terms)
-    back_mixed = exchange(mixed_own)
+            lambda a: head_outer(a[0], normed, a[1], branch),
+        ),
+    )
     tok_part, attn_gain_part = rms_back(tok_f32, scale_one, attn_full, normed_grad)
-    input_grad_own = after((resid_grad + tok_part).astype(BF16), right_grad, back_mixed)
-    back_grad = exchange(input_grad_own)
-
-    down_all = gather_chunks(down_grad, ranks)
-    left_all = gather_chunks(left_grad, ranks)
-    right_all = gather_chunks(right_grad, ranks)
-    head_all = gather_chunks(head_grad, ranks)
-
+    input_grad_own = (resid_grad + tok_part).astype(BF16)
     packed = jnp.concatenate(
         [
             attn_gain_part.reshape(groups, -1),
@@ -720,15 +806,32 @@
         ],
         axis=1,
     )
+    input_grad_own, packed, back_mixed, down_all = lax.optimization_barrier(
+        (input_grad_own, packed, back_mixed, down_all)
+    )
+    back_grad = exchange(input_grad_own)
+    packed, back_grad = lax.optimization_barrier((packed, back_grad))
+    head_terms, gate_up_out = lax.optimization_barrier((head_terms, gate_up_out))
+    head_grad = scatter(head_terms)
+
+    down_all = gather_finish(down_all, ranks)
+    gate_up_all = gather_chunks(gate_up_out, ranks)
+    head_all = gather_chunks(head_grad, ranks)
+
     summed = jnp.sum(exchange(packed), axis=0)
-    summed = jnp.sum(lax.all_gather(summed, "seq", axis=0, tiled=False), axis=0)
+    summed = summed.reshape(8, -1)
+    for bit in range(ranks.bit_length() - 1):
+        summed = summed + hop(summed, 1 << bit, ranks)
+    summed = summed.reshape(-1)
 
     def of_heads(start, width):
-        return widen([head_all], place, [(0, width)], width, start // width, ranks)
+        return widen([head_all], place, [(0, width)], width, start // width, ranks, shard)
 
     def of_tiles(side):
-        spans = [(at + side * tile, at + (side + 1) * tile) for at in range(0, f_part, 2 * tile)]
-        return widen([left_all, right_all], place, spans, f_part, 0, ranks)
+        spans = [
+            (at + side * tile, at + (side + 1) * tile) for at in range(0, 2 * f_part, 2 * tile)
+        ]
+        return widen([gate_up_all], place, spans, 2 * f_part, 0, ranks, shard)
 
     return (
         back_mixed[send_spot],
@@ -736,10 +839,10 @@
         of_heads(0, q_part),
         of_heads(q_part, k_part),
         of_heads(q_part + k_part, k_part),
-        widen([head_all], place, [(h_part, h_part + q_part)], h_part + q_part, 0, ranks),
+        widen([head_all], place, [(h_part, h_part + q_part)], h_part + q_part, 0, ranks, shard),
         of_tiles(0),
         of_tiles(1),
-        widen([down_all], place, [(0, f_part)], f_part, 0, ranks),
+        widen([down_all], place, [(0, f_part)], f_part, 0, ranks, shard),
         summed[:gain_rows],
         summed[gain_rows : 2 * gain_rows],
         summed[2 * gain_rows : 2 * gain_rows + HEAD_SIZE],

time: 1100 us -> 1050 us (0.955)
  matrix products: 219 us -> 98.5 us
  Pallas kernels: 217 us -> 318 us
  other arithmetic: 82.9 us -> 45.5 us
  blocking collectives: 39.4 us -> 8.04 us
  waiting for transfers between devices: 353 us -> 381 us
  starting transfers between devices: 79.1 us -> 90.5 us
    dot_general x27 -> x18, matrix products: 204 us -> 98.5 us  [dot(): lax.dot_general(left, right, (((left_dim,), (right_dim,)), ((), ())), pre...]
    pallas_call x0 -> x9, Pallas kernels: none -> 103 us  [the longest x8 86 us: rows_times(): pl.pallas_call(rows_kernel, out_shape=jax.ShapeDtypeStruct((rows, width),...]
    ppermute x44 -> x52, waiting for transfers between devices: 293 us -> 235 us  [hop(): return lax.ppermute(rows, 'seq', [(i, i ^ distance) for i in range(ranks)])]
    all_to_all x5, waiting for transfers between devices: 59.2 us -> 116 us  [exchange(): return lax.all_to_all(rows, 'fsdp', split_axis=0, concat_axis=0, tiled=True)]
    all_gather x1 -> x0, blocking collectives: 31.4 us -> none  [body(): summed = jnp.sum(lax.all_gather(summed, 'seq', axis=0, tiled=False), axis=0)]
    reduce_scatter x4 -> x3, waiting for transfers between devices: 0.01 us -> 20.5 us  [scatter(): lax.psum_scatter(terms.astype(BF16), 'fsdp', scatter_dimension=0, tiled=T...]
    another operation x10 -> x3, other arithmetic: 19.6 us -> 2.59 us  [the longest x1 1.58 us: body(): attended_grad = jnp.stack(attended_grad)]
    dot_general x2 -> x0, matrix products: 15.4 us -> none  [outer(): lax.dot_general(left.reshape(ranks, token_rows, features), right, (((0, 1...]
  transfers between devices with their start and end apart: 57 -> 63, of which waited for: 23 -> 26; matrix products, arithmetic and copies ran while one was open for 34% -> 20% of each run, Pallas kernels for 19% -> 29%
where the time goes in v2:
time: 1050 us; the launch traced here: 1040 us
  waiting for transfers between devices  381 us (36%)
  Pallas kernels  318 us (30%)
  matrix products  98.5 us (9%)
  starting transfers between devices  90.5 us (9%)
  local copies, waits for them, and re-layouts  87.4 us (8%)
  other arithmetic  45.5 us (4%)
  between operations  15.6 us (1%)
    ppermute x52, waiting for transfers between devices, hop(): return lax.ppermute(rows, 'seq', [(i, i ^ distance) for i in range(ranks)])  235 us
    all_to_all x5, waiting for transfers between devices, exchange(): return lax.all_to_all(rows, 'fsdp', split_axis=0, concat_axis=0, tiled=True)  116 us
    dot_general x18, matrix products, dot(): lax.dot_general(left, right, (((left_dim,), (right_dim,)), ((), ())), pre...  98.5 us
    pallas_call x8, Pallas kernels, rows_times(): pl.pallas_call(rows_kernel, out_shape=jax.ShapeDtypeStruct((rows, width),...  86 us
    pallas_call x4, Pallas kernels, up_chunk(): pl.pallas_call(functools.partial(up_kernel, tile), out_shape=(jax.ShapeDt...  57.7 us
    pallas_call x1, Pallas kernels, attend_back(): pl.pallas_call(functools.partial(attend_back_kernel, block, spans), out_s...  56.5 us
    ppermute x52, starting transfers between devices, hop(): return lax.ppermute(rows, 'seq', [(i, i ^ distance) for i in range(ranks)])  54.7 us
    pallas_call x1, Pallas kernels, attend(): pl.pallas_call(functools.partial(attend_kernel, block), out_shape=(jax.Sh...  44 us
  transfers between devices with their start and end apart: 63, of which 26 were waited for; matrix products, arithmetic and copies ran while one was open for 20% of the time, Pallas kernels for 29%

profile of v2, /device:TPU:0, one launch (start us, length us, event | category | flops | bytes accessed | tf_op | source)
XLA Modules:
  0.0 1044.4 jit_solution(4523923291796547110)
XLA Ops:
  41.0 36.0 %all-to-all-done.1 = bf16[8,64,2048]{2,1,0:T(8,128)(2,1)} async-done(((bf16[8,64,2048]{2,1,0:T(8,128)(2,1)}), bf16[8,64,2048]{2,1,0:T(8,128)(2,1)}, u32[]{:S(2)}, u32[]{:S(2)}) %all-to-all-start.1) | async-done | bytes 2097184 | tf_op jit(solution)/shard_map/all_to_all | solution.py:633
  91.9 44.7 %collective-permute-done.refs_2_.refs_3_ = bf16[512,2048]{1,0:T(8,128)(2,1)S(1)} collective-permute-done((bf16[512,2048]{1,0:T(8,128)(2,1)}, bf16[512,2048]{1,0:T(8,128)(2,1)S(1)}, u32[]{:S(2)}, u32[]{:S(2)}) %collective-permute-start) | collective-permute-done | bytes 2097184 | tf_op jit(solution)/shard_map/ppermute | solution.py:319
  145.7 18.1 %collective-permute-done.2.refs_6_ = bf16[256,2048]{1,0:T(8,128)(2,1)S(1)} collective-permute-done((bf16[256,2048]{1,0:T(8,128)(2,1)}, bf16[256,2048]{1,0:T(8,128)(2,1)S(1)}, u32[]{:S(2)}, u32[]{:S(2)}) %collective-permute-start.2) | collective-permute-done | bytes 1048608 | tf_op jit(solution)/shard_map/ppermute | solution.py:319
  192.2 44.0 %attend.1 = (bf16[4,512,512]{2,1,0:T(8,128)(2,1)S(1)}, bf16[512,2048]{1,0:T(8,128)(2,1)S(1)}, bf16[128,2048]{1,0:T(8,128)(2,1)S(1)}, bf16[128,2048]{1,0:T(8,128)(2,1)S(1)}, f32[2,8,2048]{2,1,0:T(8,128)S(1)}) custom-call(s32[8]{0:T(128)S(1)} %and_select_fusion.low_ref, s32[4]{0:T(128)S(1)} %iota_xor_fusion.order_ref.place_ref, ...), custom_call_target="tpu_custom_call" | custom-call | flops 1048576 | bytes 1048576 | tf_op jit(solution)/shard_map/attend/pallas_call | solution.py:232
  243.3 20.8 %collective-permute-done.8 = bf16[256,2048]{1,0:T(8,128)(2,1)S(1)} collective-permute-done((bf16[256,2048]{1,0:T(8,128)(2,1)S(1)}, bf16[256,2048]{1,0:T(8,128)(2,1)S(1)}, u32[]{:S(2)}, u32[]{:S(2)}) %collective-permute-start.8) | collective-permute-done | bytes 1048608 | tf_op jit(solution)/shard_map/ppermute | solution.py:319
  268.7 17.9 %collective-permute-done.6 = bf16[256,2048]{1,0:T(8,128)(2,1)S(1)} collective-permute-done((bf16[256,2048]{1,0:T(8,128)(2,1)S(1)}, bf16[256,2048]{1,0:T(8,128)(2,1)S(1)}, u32[]{:S(2)}, u32[]{:S(2)}) %collective-permute-start.6) | collective-permute-done | bytes 1048608 | tf_op jit(solution)/shard_map/ppermute | solution.py:319
  291.0 18.6 %collective-permute-done.11 = bf16[256,2048]{1,0:T(8,128)(2,1)S(1)} collective-permute-done((bf16[256,2048]{1,0:T(8,128)(2,1)S(1)}, bf16[256,2048]{1,0:T(8,128)(2,1)S(1)}, u32[]{:S(2)}, u32[]{:S(2)}) %collective-permute-start.11) | collective-permute-done | bytes 1048608 | tf_op jit(solution)/shard_map/ppermute | solution.py:319
  326.0 14.8 %up_chunk.4 = (bf16[2048,4096]{1,0:T(8,128)(2,1)}, bf16[2048,2048]{1,0:T(8,128)(2,1)}, bf16[2048,2048]{1,0:T(8,128)(2,1)}) custom-call(bf16[512,2048]{1,0:T(8,128)(2,1)S(1)} %multiply_convert_fusion.xa.xb, bf16[512,2048]{1,0:T(8,128)(2,1)S(1)} %multiply_convert_fusion.xa.xb, bf16[2048,4096]{1,0:T(8,128)(2,1)} %all-gather.6.cloned.1.call-done.w_ref.right), custom_call_target="tpu_custom_call" | custom-call | flops 1048576 | bytes 1048576 | tf_op jit(solution)/shard_map/up_chunk/pallas_call | solution.py:447
  340.7 18.1 %collective-permute-done.12.xa.xb = bf16[512,2048]{1,0:T(8,128)(2,1)} collective-permute-done((bf16[512,2048]{1,0:T(8,128)(2,1)S(1)}, bf16[512,2048]{1,0:T(8,128)(2,1)}, u32[]{:S(2)}, u32[]{:S(2)}) %collective-permute-start.12) | collective-permute-done | bytes 2097184 | tf_op jit(solution)/shard_map/ppermute | solution.py:319
  370.5 14.7 %up_chunk.5 = (bf16[2048,4096]{1,0:T(8,128)(2,1)}, bf16[2048,2048]{1,0:T(8,128)(2,1)}, bf16[2048,2048]{1,0:T(8,128)(2,1)}) custom-call(bf16[512,2048]{1,0:T(8,128)(2,1)} %collective-permute-done.12.xa.xb, bf16[512,2048]{1,0:T(8,128)(2,1)} %collective-permute-done.12.xa.xb, ...), custom_call_target="tpu_custom_call", output_to_operand_aliasing={{0}: (3, {}), {1}: (4, {}), {2}: (5, {})} | custom-call | flops 1048576 | bytes 1048576 | tf_op jit(solution)/shard_map/up_chunk/pallas_call | solution.py:447
  385.1 14.5 %up_chunk.6 = (bf16[2048,4096]{1,0:T(8,128)(2,1)}, bf16[2048,2048]{1,0:T(8,128)(2,1)}, bf16[2048,2048]{1,0:T(8,128)(2,1)}) custom-call(bf16[512,2048]{1,0:T(8,128)(2,1)} %collective-permute-done.13.xa.xb, bf16[512,2048]{1,0:T(8,128)(2,1)} %collective-permute-done.13.xa.xb, ...), custom_call_target="tpu_custom_call", output_to_operand_aliasing={{0}: (3, {}), {1}: (4, {}), {2}: (5, {})} | custom-call | flops 1048576 | bytes 1048576 | tf_op jit(solution)/shard_map/up_chunk/pallas_call | solution.py:447
  399.6 13.8 %up_chunk.7 = (bf16[2048,4096]{1,0:T(8,128)(2,1)}, bf16[2048,2048]{1,0:T(8,128)(2,1)}, bf16[2048,2048]{1,0:T(8,128)(2,1)}) custom-call(bf16[256,2048]{1,0:T(8,128)(2,1)S(1)} %collective-permute-done.14.xa, bf16[256,2048]{1,0:T(8,128)(2,1)S(1)} %collective-permute-done.15.xb, ...), custom_call_target="tpu_custom_call", output_to_operand_aliasing={{0}: (3, {}), {1}: (4, {}), {2}: (5, {})} | custom-call | flops 1048576 | bytes 1048576 | tf_op jit(solution)/shard_map/up_chunk/pallas_call | solution.py:447
  439.1 20.1 %convolution_convert_fusion.1 = bf16[2048,2048]{1,0:T(8,128)(2,1)} fusion(bf16[2048,2048]{1,0:T(8,128)(2,1)S(1)} %constant_dynamic-update-slice_fusion.c_ref, bf16[2048,2048]{1,0:T(8,128)(2,1)S(1)} %bitcast.94), kind=kOutput, calls=%fused_computation.6 | convolution fusion | flops 17184063488 | bytes 25165824 | tf_op jit(solution)/shard_map/dot_general | solution.py:26
  483.1 27.7 %hidden_back.1.left = bf16[2048,4096]{1,0:T(8,128)(2,1)} custom-call(bf16[2048,2048]{1,0:T(8,128)(2,1)} %copy-done.38, bf16[2048,2048]{1,0:T(8,128)(2,1)} %all-gather.8.cloned.1.call-done.right.w_ref, bf16[2048,4096]{1,0:T(8,128)(2,1)} %get-tuple-element.198.f_ref), custom_call_target="tpu_custom_call" | custom-call | flops 1048576 | bytes 1048576 | tf_op jit(solution)/shard_map/hidden_back/pallas_call | solution.py:529
  542.3 13.3 %rows_times.13 = bf16[512,2048]{1,0:T(8,128)(2,1)S(1)} custom-call(bf16[2048,4096]{1,0:T(8,128)(2,1)} %hidden_back.1.left, bf16[2048,4096]{1,0:T(8,128)(2,1)} %all-gather.6.cloned.1.call-done.w_ref.right), custom_call_target="tpu_custom_call" | custom-call | flops 1048576 | bytes 1048576 | tf_op jit(solution)/shard_map/rows_times/pallas_call | solution.py:404
  581.9 14.8 %collective-permute-done.25 = bf16[256,2048]{1,0:T(8,128)(2,1)S(1)} collective-permute-done((bf16[256,2048]{1,0:T(8,128)(2,1)S(1)}, bf16[256,2048]{1,0:T(8,128)(2,1)S(1)}, u32[]{:S(2)}, u32[]{:S(2)}) %collective-permute-start.25) | collective-permute-done | bytes 1048608 | tf_op jit(solution)/shard_map/ppermute | solution.py:319
  613.8 38.3 %convolution_convert_fusion = bf16[2048,4096]{1,0:T(8,128)(2,1)} fusion(bf16[2048,2048]{1,0:T(8,128)(2,1)S(1)} %bitcast.96, bf16[2048,4096]{1,0:T(8,128)(2,1)S(1)} %bitcast.92), kind=kOutput, calls=%fused_computation.5 | convolution fusion | flops 34368126976 | bytes 41943040 | tf_op jit(solution)/shard_map/dot_general | solution.py:26
  696.5 56.5 %attend_back.1 = (bf16[4,768,512]{2,1,0:T(8,128)(2,1)}, f32[2,64,128]{2,1,0:T(8,128)S(1)}) custom-call(s32[8]{0:T(128)S(1)} %copy-done.22, s32[4]{0:T(128)S(1)} %copy-done.20, f32[4,768,512]{2,1,0:T(8,128)} %copy-done.2, f32[4,768,512]{2,1,0:T(8,128)} %copy-done.2, s32[1,2048]{1,0:T(1,128)S(1)} %bitcast.90, f32[32,2048]{1,0:T(8,128)S(1)} %copy-done.10, ...), custom_call_target="tpu_custom_call" | custom-call | flops 399999991808 | bytes 1048576 | tf_op jit(solution)/shard_map/attend_back/pallas_call | solution.py:270
  766.7 17.1 %collective-permute-done.36 = bf16[256,2048]{1,0:T(8,128)(2,1)S(1)} collective-permute-done((bf16[256,2048]{1,0:T(8,128)(2,1)S(1)}, bf16[256,2048]{1,0:T(8,128)(2,1)S(1)}, u32[]{:S(2)}, u32[]{:S(2)}) %collective-permute-start.36) | collective-permute-done | bytes 1048608 | tf_op jit(solution)/shard_map/ppermute | solution.py:319
  790.1 17.0 %head_outer.1 = bf16[2048,1280]{1,0:T(8,128)(2,1)} custom-call(bf16[4,768,512]{2,1,0:T(8,128)(2,1)} %get-tuple-element.240.d_ref, bf16[4,512,512]{2,1,0:T(8,128)(2,1)} %copy-done.5, bf16[512,2048]{1,0:T(8,128)(2,1)} %fusion.4.refs_0_.refs_1_, bf16[512,2048]{1,0:T(8,128)(2,1)} %fusion.4.refs_0_.refs_1_, bf16[512,2048]{1,0:T(8,128)(2,1)} %copy-done.34, ...), custom_call_target="tpu_custom_call" | custom-call | flops 1048576 | bytes 1048576 | tf_op jit(solution)/shard_map/head_outer/pallas_call | solution.py:499
  811.2 15.3 %collective-permute-done.37 = bf16[256,2048]{1,0:T(8,128)(2,1)} collective-permute-done((bf16[256,2048]{1,0:T(8,128)(2,1)}, bf16[256,2048]{1,0:T(8,128)(2,1)}, u32[]{:S(2)}, u32[]{:S(2)}) %collective-permute-start.37) | collective-permute-done | bytes 1048608 | tf_op jit(solution)/shard_map/ppermute | solution.py:319
  831.3 20.5 %reduce-scatter.6.cloned.1.call-done.refs_0_.refs_1_ = bf16[256,4096]{1,0:T(8,128)(2,1)} async-done(((bf16[2048,4096]{1,0:T(8,128)(2,1)}), bf16[256,4096]{1,0:T(8,128)(2,1)}) %reduce-scatter.6.cloned.1.call-update) | async-done | bytes 2097168 | tf_op jit(solution)/shard_map/reduce_scatter | solution.py:721
  861.6 14.5 %all-to-all-start.4 = ((bf16[8,64,2048]{2,1,0:T(8,128)(2,1)}), bf16[8,64,2048]{2,1,0:T(8,128)(2,1)}, u32[]{:S(2)}, u32[]{:S(2)}) async-start(bf16[8,64,2048]{2,1,0:T(8,128)(2,1)} %bitcast.101), calls=%async_computation.5 | async-start | bytes 4194304 | tf_op jit(solution)/shard_map/all_to_all | solution.py:633
  884.0 73.6 %all-to-all-done.4 = bf16[8,64,2048]{2,1,0:T(8,128)(2,1)} async-done(((bf16[8,64,2048]{2,1,0:T(8,128)(2,1)}), bf16[8,64,2048]{2,1,0:T(8,128)(2,1)}, u32[]{:S(2)}, u32[]{:S(2)}) %all-to-all-start.4) | async-done | bytes 2097184 | tf_op jit(solution)/shard_map/all_to_all | solution.py:633
  (407 shorter events, 424.1 us)
Async XLA Ops:
  22.7 54.3 %all-to-all-start.1 = ((bf16[8,64,2048]{2,1,0:T(8,128)(2,1)}), bf16[8,64,2048]{2,1,0:T(8,128)(2,1)}, u32[]{:S(2)}, u32[]{:S(2)}) async-start(bf16[8,64,2048]{2,1,0:T(8,128)(2,1)} %bitcast.98), calls=%async_computation.1 | async-start | bytes 4194304 | tf_op jit(solution)/shard_map/all_to_all | solution.py:633
  27.8 148.6 %all-gather.4.cloned.1.call-start = ((), (), s32[]{:S(2)}) async-start(), calls=%async_computation.9 | async-start | bytes 5898240 | tf_op jit(solution)/shard_map/all_gather | solution.py:646
  77.0 248.9 %all-gather.6.cloned.1.call-start = ((), (), s32[]{:S(2)}) async-start(), calls=%async_computation.10 | async-start | bytes 18874368 | tf_op jit(solution)/shard_map/all_gather | solution.py:646
  77.8 95.6 %all-to-all-start.2 = ((bf16[8,64,2048]{2,1,0:T(8,128)(2,1)}), bf16[8,64,2048]{2,1,0:T(8,128)(2,1)}, u32[]{:S(2)}, u32[]{:S(2)}) async-start(bf16[8,64,2048]{2,1,0:T(8,128)(2,1)} %bitcast.2), calls=%async_computation.2 | async-start | bytes 4194304 | tf_op jit(solution)/shard_map/all_to_all | solution.py:633
  82.2 334.4 %all-gather.8.cloned.1.call-start = ((), (), s32[]{:S(2)}) async-start(), calls=%async_computation.11 | async-start | bytes 9437184 | tf_op jit(solution)/shard_map/all_gather | solution.py:646
  84.5 607.9 %reduce-scatter.4.cloned.1.call-start = ((), (), s32[]{:S(2)}) async-start(), calls=%async_computation.12 | async-start | bytes 9437184 | tf_op jit(solution)/shard_map/reduce_scatter | solution.py:721
  88.5 48.1 %collective-permute-start = (bf16[512,2048]{1,0:T(8,128)(2,1)}, bf16[512,2048]{1,0:T(8,128)(2,1)S(1)}, u32[]{:S(2)}, u32[]{:S(2)}) collective-permute-start(bf16[512,2048]{1,0:T(8,128)(2,1)} %fusion.4.refs_0_.refs_1_), channel_id=1, source_target_pairs={{0,1},{1,0},{2,3},{3,2},{4,5},{5,4},{6,7},{7,6},{8,9},{9,8},{10,11... | collective-permute-start | bytes 6291464 | tf_op jit(solution)/shard_map/ppermute | solution.py:319
  90.1 50.4 %collective-permute-start.1 = (bf16[512,2048]{1,0:T(8,128)(2,1)}, bf16[512,2048]{1,0:T(8,128)(2,1)}, u32[]{:S(2)}, u32[]{:S(2)}) collective-permute-start(bf16[512,2048]{1,0:T(8,128)(2,1)} %fusion.4.refs_0_.refs_1_), channel_id=1, source_target_pairs={{0,2},{1,3},{2,0},{3,1},{4,6},{5,7},{6,4},{7,5},{8,10},{9,11},{10,... | collective-permute-start | bytes 6291464 | tf_op jit(solution)/shard_map/ppermute | solution.py:319
  173.4 62.9 %collective-permute-start.4 = (bf16[512,2048]{1,0:T(8,128)(2,1)}, bf16[512,2048]{1,0:T(8,128)(2,1)}, u32[]{:S(2)}, u32[]{:S(2)}) collective-permute-start(bf16[512,2048]{1,0:T(8,128)(2,1)} %bitcast.3), channel_id=1, source_target_pairs={{0,1},{1,0},{2,3},{3,2},{4,5},{5,4},{6,7},{7,6},{8,9},{9,8},{10,11... | collective-permute-start | bytes 6291464 | tf_op jit(solution)/shard_map/ppermute | solution.py:319
  174.9 61.4 %collective-permute-start.5 = (bf16[512,2048]{1,0:T(8,128)(2,1)}, bf16[512,2048]{1,0:T(8,128)(2,1)}, u32[]{:S(2)}, u32[]{:S(2)}) collective-permute-start(bf16[512,2048]{1,0:T(8,128)(2,1)} %bitcast.3), channel_id=1, source_target_pairs={{0,2},{1,3},{2,0},{3,1},{4,6},{5,7},{6,4},{7,5},{8,10},{9,11},{10,... | collective-permute-start | bytes 6291464 | tf_op jit(solution)/shard_map/ppermute | solution.py:319
  315.3 45.5 %collective-permute-start.13 = (bf16[512,2048]{1,0:T(8,128)(2,1)S(1)}, bf16[512,2048]{1,0:T(8,128)(2,1)}, u32[]{:S(2)}, u32[]{:S(2)}) collective-permute-start(bf16[512,2048]{1,0:T(8,128)(2,1)S(1)} %multiply_convert_fusion.xa.xb), channel_id=1, source_target_pairs={{0,2},{1,3},{2,0},{3,1},{4,6},{5,7},{6,4},{7,5},{8,10},{9,11},{10,... | collective-permute-start | bytes 6291464 | tf_op jit(solution)/shard_map/ppermute | solution.py:319
  367.3 46.0 %collective-permute-start.18 = (bf16[256,2048]{1,0:T(8,128)(2,1)S(1)}, bf16[256,2048]{1,0:T(8,128)(2,1)}, u32[]{:S(2)}, u32[]{:S(2)}) collective-permute-start(bf16[256,2048]{1,0:T(8,128)(2,1)S(1)} %slice.192), channel_id=1, source_target_pairs={{0,2},{1,3},{2,0},{3,1},{4,6},{5,7},{6,4},{7,5},{8,10},{9,11},{10,... | collective-permute-start | bytes 3145736 | tf_op jit(solution)/shard_map/ppermute | solution.py:319
  426.6 49.5 %collective-permute-start.16 = (bf16[256,2048]{1,0:T(8,128)(2,1)}, bf16[256,2048]{1,0:T(8,128)(2,1)S(1)}, u32[]{:S(2)}, u32[]{:S(2)}) collective-permute-start(bf16[256,2048]{1,0:T(8,128)(2,1)} %get-tuple-element.281), channel_id=1, source_target_pairs={{0,2},{1,3},{2,0},{3,1},{4,6},{5,7},{6,4},{7,5},{8,10},{9,11},{10,... | collective-permute-start | bytes 3145736 | tf_op jit(solution)/shard_map/ppermute | solution.py:319
  428.3 47.8 %collective-permute-start.17 = (bf16[256,2048]{1,0:T(8,128)(2,1)}, bf16[256,2048]{1,0:T(8,128)(2,1)S(1)}, u32[]{:S(2)}, u32[]{:S(2)}) collective-permute-start(bf16[256,2048]{1,0:T(8,128)(2,1)} %get-tuple-element.280), channel_id=1, source_target_pairs={{0,1},{1,0},{2,3},{3,2},{4,5},{5,4},{6,7},{7,6},{8,9},{9,8},{10,11... | collective-permute-start | bytes 3145736 | tf_op jit(solution)/shard_map/ppermute | solution.py:319
  652.1 101.0 %all-to-all-start.3 = ((bf16[8,64,2048]{2,1,0:T(8,128)(2,1)}), bf16[8,64,2048]{2,1,0:T(8,128)(2,1)}, u32[]{:S(2)}, u32[]{:S(2)}) async-start(bf16[8,64,2048]{2,1,0:T(8,128)(2,1)} %bitcast.97), calls=%async_computation.4 | async-start | bytes 4194304 | tf_op jit(solution)/shard_map/all_to_all | solution.py:633
  656.4 195.3 %reduce-scatter.6.cloned.1.call-start = ((), (), s32[]{:S(2)}) async-start(), calls=%async_computation.13 | async-start | bytes 18874368 | tf_op jit(solution)/shard_map/reduce_scatter | solution.py:721
  664.8 330.9 %reduce-scatter.8.cloned.1.call-start = ((), (), s32[]{:S(2)}) async-start(), calls=%async_computation.14 | async-start | bytes 5898240 | tf_op jit(solution)/shard_map/reduce_scatter | solution.py:721
  692.4 60.7 %collective-permute-start.32 = (bf16[256,2048]{1,0:T(8,128)(2,1)}, bf16[256,2048]{1,0:T(8,128)(2,1)}, u32[]{:S(2)}, u32[]{:S(2)}) collective-permute-start(bf16[256,2048]{1,0:T(8,128)(2,1)} %reduce-scatter.4.cloned.1.call-done.refs_0_.refs_1_), channel_id=1, source_target_pairs={{0,1},{1,0},{2,3},{3,2},{4,5},{5,4},{6,7},{7,6},{8,9},{9,8},{10,11... | collective-permute-start | bytes 3145736 | tf_op jit(solution)/shard_map/ppermute | solution.py:319
  692.9 60.2 %collective-permute-start.33 = (bf16[256,2048]{1,0:T(8,128)(2,1)}, bf16[256,2048]{1,0:T(8,128)(2,1)}, u32[]{:S(2)}, u32[]{:S(2)}) collective-permute-start(bf16[256,2048]{1,0:T(8,128)(2,1)} %reduce-scatter.4.cloned.1.call-done.refs_0_.refs_1_), channel_id=1, source_target_pairs={{0,2},{1,3},{2,0},{3,1},{4,6},{5,7},{6,4},{7,5},{8,10},{9,11},{10,... | collective-permute-start | bytes 3145736 | tf_op jit(solution)/shard_map/ppermute | solution.py:319
  861.6 96.0 %all-to-all-start.4 = ((bf16[8,64,2048]{2,1,0:T(8,128)(2,1)}), bf16[8,64,2048]{2,1,0:T(8,128)(2,1)}, u32[]{:S(2)}, u32[]{:S(2)}) async-start(bf16[8,64,2048]{2,1,0:T(8,128)(2,1)} %bitcast.101), calls=%async_computation.5 | async-start | bytes 4194304 | tf_op jit(solution)/shard_map/all_to_all | solution.py:633
  876.1 98.8 %collective-permute-start.44 = (bf16[256,4096]{1,0:T(8,128)(2,1)S(1)}, bf16[256,4096]{1,0:T(8,128)(2,1)}, u32[]{:S(2)}, u32[]{:S(2)}) collective-permute-start(bf16[256,4096]{1,0:T(8,128)(2,1)S(1)} %copy-done.25), channel_id=1, source_target_pairs={{0,1},{1,0},{2,3},{3,2},{4,5},{5,4},{6,7},{7,6},{8,9},{9,8},{10,11... | collective-permute-start | bytes 6291464 | tf_op jit(solution)/shard_map/ppermute | solution.py:319
  876.2 101.8 %collective-permute-start.45 = (bf16[256,4096]{1,0:T(8,128)(2,1)S(1)}, bf16[256,4096]{1,0:T(8,128)(2,1)}, u32[]{:S(2)}, u32[]{:S(2)}) collective-permute-start(bf16[256,4096]{1,0:T(8,128)(2,1)S(1)} %copy-done.25), channel_id=1, source_target_pairs={{0,2},{1,3},{2,0},{3,1},{4,6},{5,7},{6,4},{7,5},{8,10},{9,11},{10,... | collective-permute-start | bytes 6291464 | tf_op jit(solution)/shard_map/ppermute | solution.py:319
  879.1 102.5 %collective-permute-start.48 = (bf16[128,2048]{1,0:T(8,128)(2,1)}, bf16[128,2048]{1,0:T(8,128)(2,1)S(1)}, u32[]{:S(2)}, u32[]{:S(2)}) collective-permute-start(bf16[128,2048]{1,0:T(8,128)(2,1)} %slice.222), channel_id=1, source_target_pairs={{0,2},{1,3},{2,0},{3,1},{4,6},{5,7},{6,4},{7,5},{8,10},{9,11},{10,... | collective-permute-start | bytes 1572872 | tf_op jit(solution)/shard_map/ppermute | solution.py:319
  882.1 99.6 %collective-permute-start.49 = (bf16[128,2048]{1,0:T(8,128)(2,1)}, bf16[128,2048]{1,0:T(8,128)(2,1)S(1)}, u32[]{:S(2)}, u32[]{:S(2)}) collective-permute-start(bf16[128,2048]{1,0:T(8,128)(2,1)} %slice.223), channel_id=1, source_target_pairs={{0,1},{1,0},{2,3},{3,2},{4,5},{5,4},{6,7},{7,6},{8,9},{9,8},{10,11... | collective-permute-start | bytes 1572872 | tf_op jit(solution)/shard_map/ppermute | solution.py:319
  (112 other events, 2406.3 us)
Sparse Core Ops, SparseCore 0:
  77.1 97.2 all-gather.3
  176.6 149.2 all-gather.5
  327.6 80.2 all-gather.7
  483.2 87.5 reduce-scatter.3
  664.9 186.7 reduce-scatter.5
  854.5 105.6 reduce-scatter.7

commit v3 on v2

--- a/solution.py
+++ b/solution.py
@@ -751,19 +751,24 @@
     factors, down_parts, cot = lax.optimization_barrier((factors, down_parts, cot))
     down_sent = [hop(part, k + 1, ranks) for k, part in enumerate(down_parts)]
     gate_up_grad = hidden_back(cot, down_own, factors, tile)
-    normed_two_grad, down_sent, down_out, _ = scatter_chunks(
+    normed_two_grad, (down_sent, left_terms), down_out, _ = scatter_chunks(
         lambda k, given: rows_times(given, k, gate_up_own, token_rows),
         gate_up_grad,
         ranks,
-        early=(down_sent, lambda a: a),
+        early=(
+            (down_sent, normed_two),
+            lambda a: (a[0], terms_of(a[1], gate_up_grad[:, :f_part])),
+        ),
         late=(hidden, lambda a: down_part(0, a)),
     )
+    left_terms, down_grad = lax.optimization_barrier((left_terms, down_grad))
+    left_out = scatter(left_terms)
     resid_part, ffn_gain_part = rms_back(resid, scale_two, ffn_full, normed_two_grad)
     resid_grad = cot_owned.astype(F32) + resid_part
     branch_own = resid_grad.astype(BF16)
     branch_own, normed_two = lax.optimization_barrier((branch_own, normed_two))
     branch = gather_start(branch_own, ranks)
-    gate_up_terms = terms_of(normed_two, gate_up_grad)
+    right_terms = terms_of(normed_two, gate_up_grad[:, f_part:])
     down_out = sum((part.astype(F32) for part in down_sent), down_out.astype(F32))
     mixed_own = (resid + down_out).astype(BF16)
 
@@ -771,19 +776,20 @@
         return dot(wo_own, rows, 0, 1).astype(BF16)
 
     attended_grad = [heads_of(rows) for rows in branch]
-    branch, gate_up_terms = lax.optimization_barrier((branch, gate_up_terms))
-    gate_up_out = scatter(gate_up_terms)
+    branch, right_terms, left_out = lax.optimization_barrier((branch, right_terms, left_out))
+    right_out = scatter(right_terms)
     branch = gather_finish(branch, ranks)
     if ranks == 4:
         attended_grad.append(heads_of(joined(branch[-1])))
     attended_grad = jnp.stack(attended_grad)
     down_all = gather_start(down_grad, ranks)
+    left_all = gather_start(left_out, ranks)
     d_heads, head_gain_parts = attend_back(
         qkv_raw, low, place, start_row, cosine, sine, head_gains, query, key, value, lse_table,
         attended, attended_grad, ranks, local, block,
     )
-    d_heads, down_all, back_mixed = lax.optimization_barrier(
-        (d_heads, down_all, exchange(mixed_own))
+    d_heads, down_all, left_all, back_mixed = lax.optimization_barrier(
+        (d_heads, down_all, left_all, exchange(mixed_own))
     )
 
     normed_grad, _, head_terms, _ = scatter_chunks(
@@ -795,6 +801,8 @@
             lambda a: head_outer(a[0], normed, a[1], branch),
         ),
     )
+    head_terms, right_out = lax.optimization_barrier((head_terms, right_out))
+    head_grad = scatter(head_terms)
     tok_part, attn_gain_part = rms_back(tok_f32, scale_one, attn_full, normed_grad)
     input_grad_own = (resid_grad + tok_part).astype(BF16)
     packed = jnp.concatenate(
@@ -810,13 +818,31 @@
         (input_grad_own, packed, back_mixed, down_all)
     )
     back_grad = exchange(input_grad_own)
-    packed, back_grad = lax.optimization_barrier((packed, back_grad))
-    head_terms, gate_up_out = lax.optimization_barrier((head_terms, gate_up_out))
-    head_grad = scatter(head_terms)
 
     down_all = gather_finish(down_all, ranks)
-    gate_up_all = gather_chunks(gate_up_out, ranks)
+    left_all = gather_finish(left_all, ranks)
+    right_all = gather_chunks(right_out, ranks)
     head_all = gather_chunks(head_grad, ranks)
+
+    def of_heads(start, width):
+        return widen([head_all], place, [(0, width)], width, start // width, ranks, shard)
+
+    def of_tiles(side):
+        spans = [
+            (at + side * tile, at + (side + 1) * tile) for at in range(0, f_part, 2 * tile)
+        ]
+        return widen([left_all, right_all], place, spans, f_part, 0, ranks, shard)
+
+    back_grad, packed, mixed, gate_out, up_out, down_out = lax.optimization_barrier(
+        (
+            back_grad,
+            packed,
+            back_mixed[send_spot],
+            of_tiles(0),
+            of_tiles(1),
+            widen([down_all], place, [(0, f_part)], f_part, 0, ranks, shard),
+        )
+    )
 
     summed = jnp.sum(exchange(packed), axis=0)
     summed = summed.reshape(8, -1)
@@ -824,25 +850,16 @@
         summed = summed + hop(summed, 1 << bit, ranks)
     summed = summed.reshape(-1)
 
-    def of_heads(start, width):
-        return widen([head_all], place, [(0, width)], width, start // width, ranks, shard)
-
-    def of_tiles(side):
-        spans = [
-            (at + side * tile, at + (side + 1) * tile) for at in range(0, 2 * f_part, 2 * tile)
-        ]
-        return widen([gate_up_all], place, spans, 2 * f_part, 0, ranks, shard)
-
     return (
-        back_mixed[send_spot],
+        mixed,
         back_grad[send_spot],
         of_heads(0, q_part),
         of_heads(q_part, k_part),
         of_heads(q_part + k_part, k_part),
         widen([head_all], place, [(h_part, h_part + q_part)], h_part + q_part, 0, ranks, shard),
-        of_tiles(0),
-        of_tiles(1),
-        widen([down_all], place, [(0, f_part)], f_part, 0, ranks, shard),
+        gate_out,
+        up_out,
+        down_out,
         summed[:gain_rows],
         summed[gain_rows : 2 * gain_rows],
         summed[2 * gain_rows : 2 * gain_rows + HEAD_SIZE],

time: 1050 us -> 1060 us (level)
  waiting for transfers between devices: 381 us -> 319 us
  starting transfers between devices: 90.5 us -> 125 us
  blocking collectives: 8.04 us -> 22.6 us
  matrix products: 98.5 us -> 110 us
    all_to_all x5, waiting for transfers between devices: 116 us -> 45.5 us  [exchange(): return lax.all_to_all(rows, 'fsdp', split_axis=0, concat_axis=0, tiled=True)]
    all_to_all x5, starting transfers between devices: 34.7 us -> 59.2 us  [exchange(): return lax.all_to_all(rows, 'fsdp', split_axis=0, concat_axis=0, tiled=True)]
    all_to_all x1, blocking collectives: 8.04 us -> 22.6 us  [exchange(): return lax.all_to_all(rows, 'fsdp', split_axis=0, concat_axis=0, tiled=True)]
    dot_general x18 -> x19, matrix products: 98.5 us -> 110 us  [dot(): lax.dot_general(left, right, (((left_dim,), (right_dim,)), ((), ())), pre...]
    ppermute x52 -> x56, starting transfers between devices: 54.7 us -> 65.6 us  [hop(): return lax.ppermute(rows, 'seq', [(i, i ^ distance) for i in range(ranks)])]
    ppermute x52 -> x56, waiting for transfers between devices: 235 us -> 245 us  [hop(): return lax.ppermute(rows, 'seq', [(i, i ^ distance) for i in range(ranks)])]
    slice x14 -> x16, local copies, waits for them, and re-layouts: 20.4 us -> 22.3 us  [gather_finish(): corner = (hop(chunks[1][:half], 2, ranks), hop(chunks[2][half:], 1, ranks))]
    unnamed x155 -> x141, local copies, waits for them, and re-layouts: 28.4 us -> 27.6 us
  transfers between devices with their start and end apart: 63 -> 68, of which waited for: 26 -> 32; matrix products, arithmetic and copies ran while one was open for 20% -> 22% of each run, Pallas kernels for 29% -> 28%
where the time goes in v3:
time: 1060 us; the launch traced here: 1050 us
  waiting for transfers between devices  319 us (30%)
  Pallas kernels  317 us (30%)
  starting transfers between devices  125 us (12%)
  matrix products  110 us (10%)
  local copies, waits for them, and re-layouts  90.1 us (8%)
  other arithmetic  51.7 us (5%)
  blocking collectives  22.6 us (2%)
  between operations  15.9 us (2%)
    ppermute x56, waiting for transfers between devices, hop(): return lax.ppermute(rows, 'seq', [(i, i ^ distance) for i in range(ranks)])  245 us
    dot_general x19, matrix products, dot(): lax.dot_general(left, right, (((left_dim,), (right_dim,)), ((), ())), pre...  110 us
    pallas_call x8, Pallas kernels, rows_times(): pl.pallas_call(rows_kernel, out_shape=jax.ShapeDtypeStruct((rows, width),...  85.2 us
    ppermute x56, starting transfers between devices, hop(): return lax.ppermute(rows, 'seq', [(i, i ^ distance) for i in range(ranks)])  65.6 us
    all_to_all x5, starting transfers between devices, exchange(): return lax.all_to_all(rows, 'fsdp', split_axis=0, concat_axis=0, tiled=True)  59.2 us
    pallas_call x4, Pallas kernels, up_chunk(): pl.pallas_call(functools.partial(up_kernel, tile), out_shape=(jax.ShapeDt...  57.8 us
    pallas_call x1, Pallas kernels, attend_back(): pl.pallas_call(functools.partial(attend_back_kernel, block, spans), out_s...  56.7 us
    all_to_all x5, waiting for transfers between devices, exchange(): return lax.all_to_all(rows, 'fsdp', split_axis=0, concat_axis=0, tiled=True)  45.5 us
  transfers between devices with their start and end apart: 68, of which 32 were waited for; matrix products, arithmetic and copies ran while one was open for 22% of the time, Pallas kernels for 28%

profile of v3, /device:TPU:0, one launch (start us, length us, event | category | flops | bytes accessed | tf_op | source)
XLA Modules:
  0.0 1052.3 jit_solution(5123801197154840450)
XLA Ops:
  41.1 35.9 %all-to-all-done.1 = bf16[8,64,2048]{2,1,0:T(8,128)(2,1)} async-done(((bf16[8,64,2048]{2,1,0:T(8,128)(2,1)}), bf16[8,64,2048]{2,1,0:T(8,128)(2,1)}, u32[]{:S(2)}, u32[]{:S(2)}) %all-to-all-start.1) | async-done | bytes 2097184 | tf_op jit(solution)/shard_map/all_to_all | solution.py:633
  91.9 44.7 %collective-permute-done.refs_2_.refs_3_ = bf16[512,2048]{1,0:T(8,128)(2,1)S(1)} collective-permute-done((bf16[512,2048]{1,0:T(8,128)(2,1)}, bf16[512,2048]{1,0:T(8,128)(2,1)S(1)}, u32[]{:S(2)}, u32[]{:S(2)}) %collective-permute-start) | collective-permute-done | bytes 2097184 | tf_op jit(solution)/shard_map/ppermute | solution.py:319
  145.7 18.2 %collective-permute-done.2.refs_6_ = bf16[256,2048]{1,0:T(8,128)(2,1)S(1)} collective-permute-done((bf16[256,2048]{1,0:T(8,128)(2,1)}, bf16[256,2048]{1,0:T(8,128)(2,1)S(1)}, u32[]{:S(2)}, u32[]{:S(2)}) %collective-permute-start.2) | collective-permute-done | bytes 1048608 | tf_op jit(solution)/shard_map/ppermute | solution.py:319
  192.4 44.0 %attend.1 = (bf16[4,512,512]{2,1,0:T(8,128)(2,1)S(1)}, bf16[512,2048]{1,0:T(8,128)(2,1)S(1)}, bf16[128,2048]{1,0:T(8,128)(2,1)S(1)}, bf16[128,2048]{1,0:T(8,128)(2,1)S(1)}, f32[2,8,2048]{2,1,0:T(8,128)S(1)}) custom-call(s32[8]{0:T(128)S(1)} %and_select_fusion.low_ref, s32[4]{0:T(128)S(1)} %iota_xor_fusion.order_ref.place_ref, ...), custom_call_target="tpu_custom_call" | custom-call | flops 1048576 | bytes 1048576 | tf_op jit(solution)/shard_map/attend/pallas_call | solution.py:232
  243.5 19.0 %collective-permute-done.8 = bf16[256,2048]{1,0:T(8,128)(2,1)S(1)} collective-permute-done((bf16[256,2048]{1,0:T(8,128)(2,1)S(1)}, bf16[256,2048]{1,0:T(8,128)(2,1)S(1)}, u32[]{:S(2)}, u32[]{:S(2)}) %collective-permute-start.8) | collective-permute-done | bytes 1048608 | tf_op jit(solution)/shard_map/ppermute | solution.py:319
  268.6 16.3 %collective-permute-done.6 = bf16[256,2048]{1,0:T(8,128)(2,1)S(1)} collective-permute-done((bf16[256,2048]{1,0:T(8,128)(2,1)S(1)}, bf16[256,2048]{1,0:T(8,128)(2,1)S(1)}, u32[]{:S(2)}, u32[]{:S(2)}) %collective-permute-start.6) | collective-permute-done | bytes 1048608 | tf_op jit(solution)/shard_map/ppermute | solution.py:319
  286.5 22.5 %collective-permute-done.11 = bf16[256,2048]{1,0:T(8,128)(2,1)S(1)} collective-permute-done((bf16[256,2048]{1,0:T(8,128)(2,1)S(1)}, bf16[256,2048]{1,0:T(8,128)(2,1)S(1)}, u32[]{:S(2)}, u32[]{:S(2)}) %collective-permute-start.11) | collective-permute-done | bytes 1048608 | tf_op jit(solution)/shard_map/ppermute | solution.py:319
  325.9 14.8 %up_chunk.4 = (bf16[2048,4096]{1,0:T(8,128)(2,1)}, bf16[2048,2048]{1,0:T(8,128)(2,1)}, bf16[2048,2048]{1,0:T(8,128)(2,1)}) custom-call(bf16[512,2048]{1,0:T(8,128)(2,1)S(1)} %multiply_convert_fusion.xa.xb, bf16[512,2048]{1,0:T(8,128)(2,1)S(1)} %multiply_convert_fusion.xa.xb, bf16[2048,4096]{1,0:T(8,128)(2,1)} %all-gather.6.cloned.1.call-done.w_ref.right), custom_call_target="tpu_custom_call" | custom-call | flops 1048576 | bytes 1048576 | tf_op jit(solution)/shard_map/up_chunk/pallas_call | solution.py:447
  340.7 20.5 %collective-permute-done.12.xa.xb = bf16[512,2048]{1,0:T(8,128)(2,1)} collective-permute-done((bf16[512,2048]{1,0:T(8,128)(2,1)S(1)}, bf16[512,2048]{1,0:T(8,128)(2,1)}, u32[]{:S(2)}, u32[]{:S(2)}) %collective-permute-start.12) | collective-permute-done | bytes 2097184 | tf_op jit(solution)/shard_map/ppermute | solution.py:319
  373.6 14.7 %up_chunk.5 = (bf16[2048,4096]{1,0:T(8,128)(2,1)}, bf16[2048,2048]{1,0:T(8,128)(2,1)}, bf16[2048,2048]{1,0:T(8,128)(2,1)}) custom-call(bf16[512,2048]{1,0:T(8,128)(2,1)} %collective-permute-done.12.xa.xb, bf16[512,2048]{1,0:T(8,128)(2,1)} %collective-permute-done.12.xa.xb, ...), custom_call_target="tpu_custom_call", output_to_operand_aliasing={{0}: (3, {}), {1}: (4, {}), {2}: (5, {})} | custom-call | flops 1048576 | bytes 1048576 | tf_op jit(solution)/shard_map/up_chunk/pallas_call | solution.py:447
  388.3 14.5 %up_chunk.6 = (bf16[2048,4096]{1,0:T(8,128)(2,1)}, bf16[2048,2048]{1,0:T(8,128)(2,1)}, bf16[2048,2048]{1,0:T(8,128)(2,1)}) custom-call(bf16[512,2048]{1,0:T(8,128)(2,1)} %collective-permute-done.13.xa.xb, bf16[512,2048]{1,0:T(8,128)(2,1)} %collective-permute-done.13.xa.xb, ...), custom_call_target="tpu_custom_call", output_to_operand_aliasing={{0}: (3, {}), {1}: (4, {}), {2}: (5, {})} | custom-call | flops 1048576 | bytes 1048576 | tf_op jit(solution)/shard_map/up_chunk/pallas_call | solution.py:447
  402.8 13.8 %up_chunk.7 = (bf16[2048,4096]{1,0:T(8,128)(2,1)}, bf16[2048,2048]{1,0:T(8,128)(2,1)}, bf16[2048,2048]{1,0:T(8,128)(2,1)}) custom-call(bf16[256,2048]{1,0:T(8,128)(2,1)S(1)} %collective-permute-done.14.xa, bf16[256,2048]{1,0:T(8,128)(2,1)S(1)} %collective-permute-done.15.xb, ...), custom_call_target="tpu_custom_call", output_to_operand_aliasing={{0}: (3, {}), {1}: (4, {}), {2}: (5, {})} | custom-call | flops 1048576 | bytes 1048576 | tf_op jit(solution)/shard_map/up_chunk/pallas_call | solution.py:447
  437.7 20.2 %convolution_convert_fusion = bf16[2048,2048]{1,0:T(8,128)(2,1)} fusion(bf16[2048,2048]{1,0:T(8,128)(2,1)S(1)} %constant_dynamic-update-slice_fusion.c_ref, bf16[2048,2048]{1,0:T(8,128)(2,1)S(1)} %bitcast.92), kind=kOutput, calls=%fused_computation.11 | convolution fusion | flops 17184063488 | bytes 25165824 | tf_op jit(solution)/shard_map/dot_general | solution.py:26
  485.5 27.0 %hidden_back.1.left = bf16[2048,4096]{1,0:T(8,128)(2,1)} custom-call(bf16[2048,2048]{1,0:T(8,128)(2,1)} %copy-done.38, bf16[2048,2048]{1,0:T(8,128)(2,1)} %all-gather.8.cloned.1.call-done.right.w_ref, bf16[2048,4096]{1,0:T(8,128)(2,1)} %get-tuple-element.210.f_ref), custom_call_target="tpu_custom_call" | custom-call | flops 1048576 | bytes 1048576 | tf_op jit(solution)/shard_map/hidden_back/pallas_call | solution.py:529
  534.5 23.8 %fusion.4 = bf16[2048,2048]{1,0:T(8,128)(2,1)} fusion(bf16[2048,2048]{1,0:T(8,128)(2,1)} %get-tuple-element.236, bf16[2048,4096]{1,0:T(8,128)(2,1)} %hidden_back.1.left), kind=kOutput, calls=%fused_computation.9 | convolution fusion | flops 17184063488 | bytes 25165824 | tf_op jit(solution)/shard_map/dot_general | solution.py:26
  618.7 19.5 %collective-permute-done.25 = bf16[256,2048]{1,0:T(8,128)(2,1)S(1)} collective-permute-done((bf16[256,2048]{1,0:T(8,128)(2,1)}, bf16[256,2048]{1,0:T(8,128)(2,1)S(1)}, u32[]{:S(2)}, u32[]{:S(2)}) %collective-permute-start.25) | collective-permute-done | bytes 1048608 | tf_op jit(solution)/shard_map/ppermute | solution.py:319
  657.8 23.9 %fusion.7 = bf16[2048,2048]{1,0:T(8,128)(2,1)} fusion(bf16[2048,2048]{1,0:T(8,128)(2,1)} %get-tuple-element.236, bf16[2048,4096]{1,0:T(8,128)(2,1)} %hidden_back.1.left), kind=kOutput, calls=%fused_computation.10 | convolution fusion | flops 17184063488 | bytes 25165824 | tf_op jit(solution)/shard_map/dot_general | solution.py:26
  681.8 14.4 %collective-permute-done.28.refs_10_.refs_11_ = bf16[512,2048]{1,0:T(8,128)(2,1)} collective-permute-done((bf16[512,2048]{1,0:T(8,128)(2,1)S(1)}, bf16[512,2048]{1,0:T(8,128)(2,1)}, u32[]{:S(2)}, u32[]{:S(2)}) %collective-permute-start.28) | collective-permute-done | bytes 2097184 | tf_op jit(solution)/shard_map/ppermute | solution.py:319
  732.3 56.7 %attend_back.1 = (bf16[4,768,512]{2,1,0:T(8,128)(2,1)}, f32[2,64,128]{2,1,0:T(8,128)S(1)}) custom-call(s32[8]{0:T(128)S(1)} %and_select_fusion.low_ref, s32[4]{0:T(128)S(1)} %iota_xor_fusion.order_ref.place_ref, f32[4,768,512]{2,1,0:T(8,128)} %copy-done.2, f32[4,768,512]{2,1,0:T(8,128)} %copy-done.2, s32[1,2048]{1,0:T(1,128)S(1)} %bitcast.90, ...), custom_call_target="tpu_custom_call" | custom-call | flops 399999991808 | bytes 1048576 | tf_op jit(solution)/shard_map/attend_back/pallas_call | solution.py:270
  816.2 17.0 %head_outer.1 = bf16[2048,1280]{1,0:T(8,128)(2,1)} custom-call(bf16[4,768,512]{2,1,0:T(8,128)(2,1)} %get-tuple-element.257.d_ref, bf16[4,512,512]{2,1,0:T(8,128)(2,1)} %copy-done.5, bf16[512,2048]{1,0:T(8,128)(2,1)} %fusion.14.refs_0_.refs_1_, bf16[512,2048]{1,0:T(8,128)(2,1)} %fusion.14.refs_0_.refs_1_, bf16[512,2048]{1,0:T(8,128)(2,1)} %copy-done.35, ...), custom_call_target="tpu_custom_call" | custom-call | flops 1048576 | bytes 1048576 | tf_op jit(solution)/shard_map/head_outer/pallas_call | solution.py:499
  837.3 16.5 %collective-permute-done.39 = bf16[256,2048]{1,0:T(8,128)(2,1)} collective-permute-done((bf16[256,2048]{1,0:T(8,128)(2,1)}, bf16[256,2048]{1,0:T(8,128)(2,1)}, u32[]{:S(2)}, u32[]{:S(2)}) %collective-permute-start.39) | collective-permute-done | bytes 1048608 | tf_op jit(solution)/shard_map/ppermute | solution.py:319
  878.3 39.0 %all-to-all-start.4 = ((bf16[8,64,2048]{2,1,0:T(8,128)(2,1)}), bf16[8,64,2048]{2,1,0:T(8,128)(2,1)}, u32[]{:S(2)}, u32[]{:S(2)}) async-start(bf16[8,64,2048]{2,1,0:T(8,128)(2,1)} %bitcast.97), calls=%async_computation.6 | async-start | bytes 4194304 | tf_op jit(solution)/shard_map/all_to_all | solution.py:633
  958.0 18.6 %reduce-scatter.11.cloned.1.call-done.refs_0_.refs_1_ = bf16[256,1280]{1,0:T(8,128)(2,1)} async-done(((bf16[2048,1280]{1,0:T(8,128)(2,1)}), bf16[256,1280]{1,0:T(8,128)(2,1)}) %reduce-scatter.11.cloned.1.call-update) | async-done | bytes 655376 | tf_op jit(solution)/shard_map/reduce_scatter | solution.py:721
  992.5 22.6 %all_to_all.63 = f32[8,1,640]{2,1,0:T(1,128)S(1)} all-to-all(f32[8,1,640]{2,1,0:T(1,128)S(1)} %all_to_all.55), channel_id=1, replica_groups=mesh['fsdp'=8,'seq'=4] {'fsdp'}, dimensions={0} | all-to-all | bytes 40960 | tf_op jit(solution)/shard_map/all_to_all | solution.py:633
  (404 shorter events, 458.3 us)
Async XLA Ops:
  22.7 54.3 %all-to-all-start.1 = ((bf16[8,64,2048]{2,1,0:T(8,128)(2,1)}), bf16[8,64,2048]{2,1,0:T(8,128)(2,1)}, u32[]{:S(2)}, u32[]{:S(2)}) async-start(bf16[8,64,2048]{2,1,0:T(8,128)(2,1)} %bitcast.94), calls=%async_computation.1 | async-start | bytes 4194304 | tf_op jit(solution)/shard_map/all_to_all | solution.py:633
  27.8 148.6 %all-gather.4.cloned.1.call-start = ((), (), s32[]{:S(2)}) async-start(), calls=%async_computation.10 | async-start | bytes 5898240 | tf_op jit(solution)/shard_map/all_gather | solution.py:646
  77.0 248.9 %all-gather.6.cloned.1.call-start = ((), (), s32[]{:S(2)}) async-start(), calls=%async_computation.11 | async-start | bytes 18874368 | tf_op jit(solution)/shard_map/all_gather | solution.py:646
  77.8 95.6 %all-to-all-start.2 = ((bf16[8,64,2048]{2,1,0:T(8,128)(2,1)}), bf16[8,64,2048]{2,1,0:T(8,128)(2,1)}, u32[]{:S(2)}, u32[]{:S(2)}) async-start(bf16[8,64,2048]{2,1,0:T(8,128)(2,1)} %bitcast.2), calls=%async_computation.2 | async-start | bytes 4194304 | tf_op jit(solution)/shard_map/all_to_all | solution.py:633
  82.2 337.6 %all-gather.8.cloned.1.call-start = ((), (), s32[]{:S(2)}) async-start(), calls=%async_computation.12 | async-start | bytes 9437184 | tf_op jit(solution)/shard_map/all_gather | solution.py:646
  84.5 507.8 %reduce-scatter.5.cloned.1.call-start = ((), (), s32[]{:S(2)}) async-start(), calls=%async_computation.13 | async-start | bytes 9437184 | tf_op jit(solution)/shard_map/reduce_scatter | solution.py:721
  173.4 63.1 %collective-permute-start.4 = (bf16[512,2048]{1,0:T(8,128)(2,1)}, bf16[512,2048]{1,0:T(8,128)(2,1)}, u32[]{:S(2)}, u32[]{:S(2)}) collective-permute-start(bf16[512,2048]{1,0:T(8,128)(2,1)} %bitcast.3), channel_id=1, source_target_pairs={{0,1},{1,0},{2,3},{3,2},{4,5},{5,4},{6,7},{7,6},{8,9},{9,8},{10,11... | collective-permute-start | bytes 6291464 | tf_op jit(solution)/shard_map/ppermute | solution.py:319
  174.9 61.6 %collective-permute-start.5 = (bf16[512,2048]{1,0:T(8,128)(2,1)}, bf16[512,2048]{1,0:T(8,128)(2,1)}, u32[]{:S(2)}, u32[]{:S(2)}) collective-permute-start(bf16[512,2048]{1,0:T(8,128)(2,1)} %bitcast.3), channel_id=1, source_target_pairs={{0,2},{1,3},{2,0},{3,1},{4,6},{5,7},{6,4},{7,5},{8,10},{9,11},{10,... | collective-permute-start | bytes 6291464 | tf_op jit(solution)/shard_map/ppermute | solution.py:319
  475.1 221.3 %reduce-scatter.7.cloned.1.call-start = ((), (), s32[]{:S(2)}) async-start(), calls=%async_computation.14 | async-start | bytes 9437184 | tf_op jit(solution)/shard_map/reduce_scatter | solution.py:721
  532.5 54.6 %collective-permute-start.24 = (bf16[256,2048]{1,0:T(8,128)(2,1)}, bf16[256,2048]{1,0:T(8,128)(2,1)}, u32[]{:S(2)}, u32[]{:S(2)}) collective-permute-start(bf16[256,2048]{1,0:T(8,128)(2,1)} %get-tuple-element.302), channel_id=1, source_target_pairs={{0,1},{1,0},{2,3},{3,2},{4,5},{5,4},{6,7},{7,6},{8,9},{9,8},{10,11... | collective-permute-start | bytes 3145736 | tf_op jit(solution)/shard_map/ppermute | solution.py:319
  533.0 56.7 %collective-permute-start.23 = (bf16[256,2048]{1,0:T(8,128)(2,1)}, bf16[256,2048]{1,0:T(8,128)(2,1)}, u32[]{:S(2)}, u32[]{:S(2)}) collective-permute-start(bf16[256,2048]{1,0:T(8,128)(2,1)} %get-tuple-element.303), channel_id=1, source_target_pairs={{0,2},{1,3},{2,0},{3,1},{4,6},{5,7},{6,4},{7,5},{8,10},{9,11},{10,... | collective-permute-start | bytes 3145736 | tf_op jit(solution)/shard_map/ppermute | solution.py:319
  653.4 135.6 %all-to-all-start.3 = ((bf16[8,64,2048]{2,1,0:T(8,128)(2,1)}), bf16[8,64,2048]{2,1,0:T(8,128)(2,1)}, u32[]{:S(2)}, u32[]{:S(2)}) async-start(bf16[8,64,2048]{2,1,0:T(8,128)(2,1)} %bitcast.93), calls=%async_computation.5 | async-start | bytes 4194304 | tf_op jit(solution)/shard_map/all_to_all | solution.py:633
  657.8 196.0 %reduce-scatter.9.cloned.1.call-start = ((), (), s32[]{:S(2)}) async-start(), calls=%async_computation.15 | async-start | bytes 9437184 | tf_op jit(solution)/shard_map/reduce_scatter | solution.py:721
  712.4 76.6 %collective-permute-start.32 = (bf16[256,2048]{1,0:T(8,128)(2,1)}, bf16[256,2048]{1,0:T(8,128)(2,1)}, u32[]{:S(2)}, u32[]{:S(2)}) collective-permute-start(bf16[256,2048]{1,0:T(8,128)(2,1)} %reduce-scatter.5.cloned.1.call-done.refs_0_.refs_1_), channel_id=1, source_target_pairs={{0,1},{1,0},{2,3},{3,2},{4,5},{5,4},{6,7},{7,6},{8,9},{9,8},{10,11... | collective-permute-start | bytes 3145736 | tf_op jit(solution)/shard_map/ppermute | solution.py:319
  713.3 75.7 %collective-permute-start.33 = (bf16[256,2048]{1,0:T(8,128)(2,1)}, bf16[256,2048]{1,0:T(8,128)(2,1)}, u32[]{:S(2)}, u32[]{:S(2)}) collective-permute-start(bf16[256,2048]{1,0:T(8,128)(2,1)} %reduce-scatter.5.cloned.1.call-done.refs_0_.refs_1_), channel_id=1, source_target_pairs={{0,2},{1,3},{2,0},{3,1},{4,6},{5,7},{6,4},{7,5},{8,10},{9,11},{10,... | collective-permute-start | bytes 3145736 | tf_op jit(solution)/shard_map/ppermute | solution.py:319
  714.8 74.3 %collective-permute-start.34 = (bf16[256,2048]{1,0:T(8,128)(2,1)}, bf16[256,2048]{1,0:T(8,128)(2,1)}, u32[]{:S(2)}, u32[]{:S(2)}) collective-permute-start(bf16[256,2048]{1,0:T(8,128)(2,1)} %reduce-scatter.7.cloned.1.call-done.refs_0_.refs_1_), channel_id=1, source_target_pairs={{0,1},{1,0},{2,3},{3,2},{4,5},{5,4},{6,7},{7,6},{8,9},{9,8},{10,11... | collective-permute-start | bytes 3145736 | tf_op jit(solution)/shard_map/ppermute | solution.py:319
  716.2 260.4 %reduce-scatter.11.cloned.1.call-start = ((), (), s32[]{:S(2)}) async-start(), calls=%async_computation.16 | async-start | bytes 5898240 | tf_op jit(solution)/shard_map/reduce_scatter | solution.py:721
  722.4 66.6 %collective-permute-start.35 = (bf16[256,2048]{1,0:T(8,128)(2,1)}, bf16[256,2048]{1,0:T(8,128)(2,1)}, u32[]{:S(2)}, u32[]{:S(2)}) collective-permute-start(bf16[256,2048]{1,0:T(8,128)(2,1)} %reduce-scatter.7.cloned.1.call-done.refs_0_.refs_1_), channel_id=1, source_target_pairs={{0,2},{1,3},{2,0},{3,1},{4,6},{5,7},{6,4},{7,5},{8,10},{9,11},{10,... | collective-permute-start | bytes 3145736 | tf_op jit(solution)/shard_map/ppermute | solution.py:319
  857.8 66.7 %collective-permute-start.44 = (bf16[256,2048]{1,0:T(8,128)(2,1)}, bf16[256,2048]{1,0:T(8,128)(2,1)}, u32[]{:S(2)}, u32[]{:S(2)}) collective-permute-start(bf16[256,2048]{1,0:T(8,128)(2,1)} %reduce-scatter.9.cloned.1.call-done.refs_8_.refs_9_), channel_id=1, source_target_pairs={{0,1},{1,0},{2,3},{3,2},{4,5},{5,4},{6,7},{7,6},{8,9},{9,8},{10,11... | collective-permute-start | bytes 3145736 | tf_op jit(solution)/shard_map/ppermute | solution.py:319
  857.9 69.3 %collective-permute-start.45 = (bf16[256,2048]{1,0:T(8,128)(2,1)}, bf16[256,2048]{1,0:T(8,128)(2,1)}, u32[]{:S(2)}, u32[]{:S(2)}) collective-permute-start(bf16[256,2048]{1,0:T(8,128)(2,1)} %reduce-scatter.9.cloned.1.call-done.refs_8_.refs_9_), channel_id=1, source_target_pairs={{0,2},{1,3},{2,0},{3,1},{4,6},{5,7},{6,4},{7,5},{8,10},{9,11},{10,... | collective-permute-start | bytes 3145736 | tf_op jit(solution)/shard_map/ppermute | solution.py:319
  869.8 59.1 %collective-permute-start.48 = (bf16[128,2048]{1,0:T(8,128)(2,1)}, bf16[128,2048]{1,0:T(8,128)(2,1)S(1)}, u32[]{:S(2)}, u32[]{:S(2)}) collective-permute-start(bf16[128,2048]{1,0:T(8,128)(2,1)} %slice.236), channel_id=1, source_target_pairs={{0,2},{1,3},{2,0},{3,1},{4,6},{5,7},{6,4},{7,5},{8,10},{9,11},{10,... | collective-permute-start | bytes 1572872 | tf_op jit(solution)/shard_map/ppermute | solution.py:319
  871.7 57.7 %collective-permute-start.49 = (bf16[128,2048]{1,0:T(8,128)(2,1)}, bf16[128,2048]{1,0:T(8,128)(2,1)S(1)}, u32[]{:S(2)}, u32[]{:S(2)}) collective-permute-start(bf16[128,2048]{1,0:T(8,128)(2,1)} %slice.237), channel_id=1, source_target_pairs={{0,1},{1,0},{2,3},{3,2},{4,5},{5,4},{6,7},{7,6},{8,9},{9,8},{10,11... | collective-permute-start | bytes 1572872 | tf_op jit(solution)/shard_map/ppermute | solution.py:319
  874.4 61.1 %collective-permute-start.42 = (bf16[128,2048]{1,0:T(8,128)(2,1)S(1)}, bf16[128,2048]{1,0:T(8,128)(2,1)S(1)}, u32[]{:S(2)}, u32[]{:S(2)}) collective-permute-start(bf16[128,2048]{1,0:T(8,128)(2,1)S(1)} %slice.232), channel_id=1, source_target_pairs={{0,2},{1,3},{2,0},{3,1},{4,6},{5,7},{6,4},{7,5},{8,10},{9,11},{10,... | collective-permute-start | bytes 1572872 | tf_op jit(solution)/shard_map/ppermute | solution.py:319
  878.3 114.1 %all-to-all-start.4 = ((bf16[8,64,2048]{2,1,0:T(8,128)(2,1)}), bf16[8,64,2048]{2,1,0:T(8,128)(2,1)}, u32[]{:S(2)}, u32[]{:S(2)}) async-start(bf16[8,64,2048]{2,1,0:T(8,128)(2,1)} %bitcast.97), calls=%async_computation.6 | async-start | bytes 4194304 | tf_op jit(solution)/shard_map/all_to_all | solution.py:633
  (109 other events, 3228.0 us)
Sparse Core Ops, SparseCore 0:
  77.1 97.2 all-gather.3
  176.6 149.2 all-gather.5
  327.6 80.2 all-gather.7
  475.3 88.1 reduce-scatter.4
  592.5 101.7 reduce-scatter.6
  716.3 106.9 reduce-scatter.8
  854.0 122.6 reduce-scatter.10
